TPU v7x, 512 devices: a whole 4x8x8 slice. The times are simulated.
512 devices in a mesh: row: 16 (over z, core), col: 32 (over x, y).
Axes of the slice: x: 4, y: 8, z: 8, core: 2. Of those that a mesh axis runs over, the one named last changes fastest.
Arguments:
- panel: bfloat16 [64, 1024, 256], P('row', 'col'), may hold values from -6 to 6
- inverse_factor: bfloat16 [1024, 1024], P('row', 'col'), as said below
- ranks: int32 [64], replicated, may hold values from 32 to 256
Outputs:
- solved: bfloat16 [64, 1024, 256], P('row', 'col')
- core_blocks: bfloat16 [64, 64, 256, 256], P('row', 'col')
Inputs may be any that keep to these rules, and one draw needn't show every extreme that they name: inverse_factor is lower triangular with a diagonal between 0.5 and 3.
All inputs are finite; a program needn't handle non-finite values.
Results may differ from a plain program's by a relative error of at most 0.017.
Values may be sent and summed in bfloat16 or wider, within the bound.
No kernel may reach another device: no remote copies, remote signals or barrier semaphores. Data moves between devices by JAX's collectives and lax.ppermute only.
A program may use at most 64 MiB of HBM per device.

v0:
```python
import jax
import jax.numpy as jnp
from jax import lax
from jax.experimental import pallas as pl
from jax.experimental.pallas import tpu as pltpu
from jax.sharding import Mesh
from jax.sharding import PartitionSpec as P


ROW = ("z", "core")
COL = ("x", "y")
ALL = ROW + COL


def size_of(axes):
    axes = axes if isinstance(axes, tuple) else (axes,)
    count = 1
    for axis in axes:
        count *= lax.axis_size(axis)
    return count


def copies_for(value, axes):
    return jnp.broadcast_to(value, (size_of(axes), *value.shape))


def exchanged(copies, axes):
    return lax.all_to_all(copies, axes, split_axis=0, concat_axis=0, tiled=True)


def column_tiles(panel, col, rows, cols):
    odd = lax.rem(col, 2)
    pair = panel.shape[0] // 2

    def moved(flip):
        half = lax.bitwise_xor(odd, flip)
        part = lax.dynamic_slice_in_dim(panel, pair * half, pair, 0)
        pairs = [
            (r * cols + c, (c // 2) * cols + 2 * r + ((c % 2) ^ flip))
            for r in range(rows)
            for c in range(cols)
        ]
        return lax.ppermute(part, ALL, pairs)

    first, second = moved(0), moved(1)
    low = jnp.where(odd == 0, first, second)
    high = jnp.where(odd == 0, second, first)
    return jnp.concatenate([low, high], axis=1)


NEAR = (0, 2, 6, 4)
ODD = (1, 3, 7, 5)
STEP = 256
IN_VMEM = pl.BlockSpec(memory_space=pltpu.VMEM)
IN_SMEM = pl.BlockSpec(memory_space=pltpu.SMEM)
IN_PLACE = pl.BlockSpec(memory_space=pl.ANY)
WHOLE_VMEM = pltpu.CompilerParams(vmem_limit_bytes=62 << 20)


def columns_kept(rank, width):
    lane = lax.broadcasted_iota(jnp.int32, (1, width), 1)
    return (lane < rank).astype(jnp.bfloat16)


def solve_block(factor, known_rows, keep, i):
    block = jnp.dot(
        factor[pl.ds(STEP * i, STEP), : STEP * (i + 1)],
        known_rows,
        preferred_element_type=jnp.float32,
    )
    return block.astype(jnp.bfloat16) * keep


def column_kernel(ranks, near, near_core, odd, odd_core, factor, solved, values):
    order, across = solved.shape
    height = near.shape[1]
    pair = values.shape[0]
    width = across // pair
    steps = order // STEP
    col = lax.axis_index(COL)
    level = lax.axis_index("z")
    core = lax.axis_index("core")
    levels = lax.axis_size("z")
    for source, shifts, k in (
        (near, NEAR, core),
        (near_core, NEAR, 1 - core),
        (odd, ODD, core),
        (odd_core, ODD, 1 - core),
    ):
        for n, shift in enumerate(shifts):
            row = 2 * lax.rem(level + shift, levels) + k
            place = pl.ds(pl.multiple_of(height * row, height), height)
            factor[place, :] = source[n, :, :order]
            for u in range(pair):
                values[u, place, :] = source[n, :, order + width * u : order + width * (u + 1)]

    for u in range(pair):
        keep = columns_kept(ranks[col * pair + u], width)
        for i in range(steps):
            solved[pl.ds(STEP * i, STEP), width * u : width * (u + 1)] = solve_block(
                factor, values[u, : STEP * (i + 1), :], keep, i
            )


def solve_columns(ranks, near, near_core, odd, odd_core, pair, width, order):
    return pl.pallas_call(
        column_kernel,
        out_shape=(
            jax.ShapeDtypeStruct((order, order), jnp.bfloat16),
            jax.ShapeDtypeStruct((order, pair * width), jnp.bfloat16),
        ),
        in_specs=[IN_SMEM] + [IN_VMEM] * 4,
        out_specs=(IN_VMEM, IN_VMEM),
        scratch_shapes=[pltpu.VMEM((pair, order, width), jnp.bfloat16)],
        compiler_params=pltpu.CompilerParams(vmem_limit_bytes=16 << 20),
        cost_estimate=pl.CostEstimate(
            flops=2 * order * order * width * pair, bytes_accessed=6 << 20, transcendentals=0
        ),
    )(ranks, near, near_core, odd, odd_core)


def row_kernel(
    ranks, factor_in, others_in, full, shares, core_blocks, factor, others, values, solved, sems
):
    _, tiles, depth, width = full.shape
    order, across = others.shape
    row = lax.axis_index(ROW)
    col = lax.axis_index(COL)
    steps = order // STEP

    def factor_rows(i):
        block = pl.ds(STEP * i, STEP)
        return pltpu.make_async_copy(factor_in.at[block, :], factor.at[block, :], sems.at[i])

    def tile_values(t):
        return pltpu.make_async_copy(full.at[:, t], values.at[t], sems.at[steps + t])

    all_others = pltpu.make_async_copy(others_in, others, sems.at[steps + tiles])

    tile_values(0).start()
    for i in range(steps):
        factor_rows(i).start()
    all_others.start()
    for t in range(1, tiles):
        tile_values(t).start()

    def one(t, first):
        tile_values(t).wait()
        keep = columns_kept(ranks[row * tiles + t], width)
        for i in range(steps):
            if first:
                factor_rows(i).wait()
            known = STEP * (i + 1)
            solved[pl.ds(STEP * i, STEP), :] = solve_block(
                factor, values[t, : known // depth].reshape(known, width), keep, i
            )
        shares[t] = solved[pl.ds(pl.multiple_of(col * depth, depth), depth), :]
        if first:
            all_others.wait()
        paired = lax.dot_general(
            solved[...],
            others[...],
            (((0,), (0,)), ((), ())),
            preferred_element_type=jnp.float32,
        ).astype(jnp.bfloat16)
        for u in range(across // width):
            core_blocks[t, u] = paired[:, width * u : width * (u + 1)]

    def later(t, carry):
        one(t, False)
        return carry

    one(0, True)
    lax.fori_loop(1, tiles, later, 0)


def solve_rows(ranks, factor, others, full):
    cols, tiles, depth, width = full.shape
    order, across = others.shape
    return pl.pallas_call(
        row_kernel,
        out_shape=(
            jax.ShapeDtypeStruct((tiles, depth, width), jnp.bfloat16),
            jax.ShapeDtypeStruct((tiles, across // width, width, width), jnp.bfloat16),
        ),
        in_specs=[IN_SMEM, IN_PLACE, IN_PLACE, IN_PLACE],
        out_specs=(IN_VMEM, IN_VMEM),
        scratch_shapes=[
            pltpu.VMEM((order, order), jnp.bfloat16),
            pltpu.VMEM((order, across), jnp.bfloat16),
            pltpu.VMEM((tiles, cols, depth, width), jnp.bfloat16),
            pltpu.VMEM((order, width), jnp.bfloat16),
            pltpu.SemaphoreType.DMA((order // STEP + tiles + 1,)),
        ],
        compiler_params=WHOLE_VMEM,
        cost_estimate=pl.CostEstimate(
            flops=3 * order * order * width * tiles, bytes_accessed=6 << 20, transcendentals=0
        ),
    )(ranks, factor, others, full)


def from_level(value, shift):
    levels = lax.axis_size("z")
    return lax.ppermute(value, "z", [((z + shift) % levels, z) for z in range(levels)])


def other_core(value):
    return lax.ppermute(value, "core", [(0, 1), (1, 0)])


def per_device(panel, inverse_factor, ranks):
    tiles, depth, width = panel.shape
    col = lax.axis_index(COL)
    rows, cols = size_of(ROW), size_of(COL)
    pair = tiles * rows // cols
    order = cols * depth

    part = column_tiles(panel, col, rows, cols)
    factor = copies_for(inverse_factor.T, COL)
    factor = exchanged(factor, COL)
    factor = factor.reshape(order, -1).T
    packed = jnp.concatenate([factor, *part], axis=1)[None]

    copies = copies_for(panel, COL)
    copies, packed = lax.optimization_barrier((copies, packed))
    full = exchanged(copies, COL)
    opposite, above, below = from_level(packed, 4), from_level(packed, 2), from_level(packed, 6)
    near = jnp.concatenate([packed, above, below, opposite])
    upper, lower = jnp.concatenate([packed, above]), jnp.concatenate([packed, below])
    upper = from_level(upper, 1)
    lower = from_level(lower, 7)
    odd = jnp.concatenate([upper, lower])
    near_core = other_core(near)
    factor, others = solve_columns(
        ranks, near, near_core, odd, other_core(odd), pair, width, order
    )
    return solve_rows(ranks, factor, others, full)


def solution(mesh):
    split = Mesh(mesh.devices.reshape(8, 2, 4, 8), ALL)
    return jax.shard_map(
        per_device,
        mesh=split,
        in_specs=(P(ROW, COL, None), P(ROW, COL), P()),
        out_specs=(P(ROW, COL, None), P(ROW, COL, None, None)),
        check_vma=False,
    )
```

profile of v0, /device:TPU:1, one launch (start us, length us, event | category | flops | bytes accessed | tf_op | source)
XLA Modules:
  0.0 103.4 jit_solution(2090667686339222194)
XLA Ops:
  0.7 0.8 constant_dynamic-slice_fusion.1
  1.5 5.6 %collective-permute-start = (bf16[2,32,256]{2,1,0:T(8,128)(2,1)S(1)}, bf16[2,32,256]{2,1,0:T(8,128)(2,1)S(1)}, u32[]{:S(2)}, u32[]{:S(2)}) collective-permute-start(bf16[2,32,256]{2,1,0:T(8,128)(2,1)S(1)} %get-tuple-element.16), channel_id=1, source_target_pairs={{0,0},{1,1},{2,32},{3,33},{4,64},{5,65},{6,96},{7,97},{8,128},{9,1... | collective-permute-start | bytes 98312 | tf_op jit(solution)/shard_map/ppermute | solution.py:43
  7.1 2.9 %collective-permute-start.1 = (bf16[2,32,256]{2,1,0:T(8,128)(2,1)S(1)}, bf16[2,32,256]{2,1,0:T(8,128)(2,1)S(1)}, u32[]{:S(2)}, u32[]{:S(2)}) collective-permute-start(bf16[2,32,256]{2,1,0:T(8,128)(2,1)S(1)} %get-tuple-element.17), channel_id=1, source_target_pairs={{0,1},{1,0},{2,33},{3,32},{4,65},{5,64},{6,97},{7,96},{8,129},{9,1... | collective-permute-start | bytes 98312 | tf_op jit(solution)/shard_map/ppermute | solution.py:43
  10.0 0.7 broadcast_in_dim.10
  10.7 0.8 reshape.8
  11.6 15.9 %all-to-all-start = ((bf16[32,2,1024]{2,1,0:T(2,128)(2,1)}), bf16[32,2,1024]{2,1,0:T(2,128)(2,1)S(1)}, u32[]{:S(2)}, u32[]{:S(2)}) async-start(bf16[32,2,1024]{2,1,0:T(2,128)(2,1)} %reshape.8), calls=%async_computation | async-start | bytes 262144 | tf_op jit(solution)/shard_map/all_to_all | solution.py:28
  27.5 0.0 collective-permute-done
  27.5 0.0 collective-permute-done.1
  27.6 9.1 %all-to-all-done = bf16[32,2,1024]{2,1,0:T(2,128)(2,1)S(1)} async-done(((bf16[32,2,1024]{2,1,0:T(2,128)(2,1)}), bf16[32,2,1024]{2,1,0:T(2,128)(2,1)S(1)}, u32[]{:S(2)}, u32[]{:S(2)}) %all-to-all-start) | async-done | bytes 131104 | tf_op jit(solution)/shard_map/all_to_all | solution.py:28
  36.7 0.2 reshape.9
  36.9 0.1 copy.6
  37.1 1.6 %broadcast_in_dim.9 = bf16[32,4,32,256]{3,2,1,0:T(8,128)(2,1)} broadcast(bf16[4,32,256]{2,1,0:T(8,128)(2,1)S(1)} %copy-done.3), dimensions={1,2,3} | broadcast | bytes 2162688 | tf_op jit(solution)/shard_map/broadcast_in_dim | solution.py:24
  38.7 4.8 %all-to-all-start.1 = ((bf16[32,4,32,256]{3,2,1,0:T(8,128)(2,1)}), bf16[32,4,32,256]{3,2,1,0:T(8,128)(2,1)}, u32[]{:S(2)}, u32[]{:S(2)}) async-start(bf16[32,4,32,256]{3,2,1,0:T(8,128)(2,1)} %broadcast_in_dim.9), calls=%async_computation.1 | async-start | bytes 4194304 | tf_op jit(solution)/shard_map/all_to_all | solution.py:28
  43.5 8.2 %collective-permute-start.4 = (bf16[1,64,1536]{2,1,0:T(8,128)(2,1)S(1)}, bf16[1,64,1536]{2,1,0:T(8,128)(2,1)S(1)}, u32[]{:S(2)}, u32[]{:S(2)}) collective-permute-start(bf16[1,64,1536]{2,1,0:T(8,128)(2,1)S(1)} %maximum_bitcast_fusion), channel_id=1, source_target_pairs={{256,0},{320,64},{384,128},{448,192},{0,256},{64,320},{128,384},{1... | collective-permute-start | bytes 589832 | tf_op jit(solution)/shard_map/ppermute | solution.py:204
  51.7 4.9 %collective-permute-start.3 = (bf16[1,64,1536]{2,1,0:T(8,128)(2,1)S(1)}, bf16[1,64,1536]{2,1,0:T(8,128)(2,1)S(1)}, u32[]{:S(2)}, u32[]{:S(2)}) collective-permute-start(bf16[1,64,1536]{2,1,0:T(8,128)(2,1)S(1)} %maximum_bitcast_fusion), channel_id=1, source_target_pairs={{384,0},{448,64},{0,128},{64,192},{128,256},{192,320},{256,384},{3... | collective-permute-start | bytes 589832 | tf_op jit(solution)/shard_map/ppermute | solution.py:204
  56.6 2.5 %collective-permute-start.2 = (bf16[1,64,1536]{2,1,0:T(8,128)(2,1)S(1)}, bf16[1,64,1536]{2,1,0:T(8,128)(2,1)S(1)}, u32[]{:S(2)}, u32[]{:S(2)}) collective-permute-start(bf16[1,64,1536]{2,1,0:T(8,128)(2,1)S(1)} %maximum_bitcast_fusion), channel_id=1, source_target_pairs={{128,0},{192,64},{256,128},{320,192},{384,256},{448,320},{0,384},{... | collective-permute-start | bytes 589832 | tf_op jit(solution)/shard_map/ppermute | solution.py:204
  59.1 0.0 copy-start
  59.1 5.0 %collective-permute-done.3 = bf16[1,64,1536]{2,1,0:T(8,128)(2,1)S(1)} collective-permute-done((bf16[1,64,1536]{2,1,0:T(8,128)(2,1)S(1)}, bf16[1,64,1536]{2,1,0:T(8,128)(2,1)S(1)}, u32[]{:S(2)}, u32[]{:S(2)}) %collective-permute-start.3) | collective-permute-done | bytes 196640 | tf_op jit(solution)/shard_map/ppermute | solution.py:204
  64.1 6.5 %collective-permute-done.2 = bf16[1,64,1536]{2,1,0:T(8,128)(2,1)S(1)} collective-permute-done((bf16[1,64,1536]{2,1,0:T(8,128)(2,1)S(1)}, bf16[1,64,1536]{2,1,0:T(8,128)(2,1)S(1)}, u32[]{:S(2)}, u32[]{:S(2)}) %collective-permute-start.2) | collective-permute-done | bytes 196640 | tf_op jit(solution)/shard_map/ppermute | solution.py:204
  70.6 0.1 pad_maximum_fusion
  70.7 2.3 %collective-permute-start.7 = (bf16[2,64,1536]{2,1,0:T(8,128)(2,1)S(1)}, bf16[2,64,1536]{2,1,0:T(8,128)(2,1)S(1)}, u32[]{:S(2)}, u32[]{:S(2)}) collective-permute-start(bf16[2,64,1536]{2,1,0:T(8,128)(2,1)S(1)} %get-tuple-element.10), channel_id=1, source_target_pairs={{448,0},{0,64},{64,128},{128,192},{192,256},{256,320},{320,384},{3... | collective-permute-start | bytes 1179656 | tf_op jit(solution)/shard_map/ppermute | solution.py:204
  73.0 4.2 %collective-permute-start.6 = (bf16[2,64,1536]{2,1,0:T(8,128)(2,1)S(1)}, bf16[2,64,1536]{2,1,0:T(8,128)(2,1)S(1)}, u32[]{:S(2)}, u32[]{:S(2)}) collective-permute-start(bf16[2,64,1536]{2,1,0:T(8,128)(2,1)S(1)} %get-tuple-element.11), channel_id=1, source_target_pairs={{64,0},{128,64},{192,128},{256,192},{320,256},{384,320},{448,384},... | collective-permute-start | bytes 1179656 | tf_op jit(solution)/shard_map/ppermute | solution.py:204
  77.2 0.0 collective-permute-done.4
  77.2 3.5 %collective-permute-start.5 = (bf16[4,64,1536]{2,1,0:T(8,128)(2,1)S(1)}, bf16[4,64,1536]{2,1,0:T(8,128)(2,1)S(1)}, u32[]{:S(2)}, u32[]{:S(2)}) collective-permute-start(bf16[4,64,1536]{2,1,0:T(8,128)(2,1)S(1)} %constant_dynamic-update-slice_fusion.near), channel_id=1, source_target_pairs={{0,32},{32,0},{1,33},{33,1},{2,34},{34,2},{3,35},{35,3},{4,36},{36... | collective-permute-start | bytes 2359304 | tf_op jit(solution)/shard_map/ppermute | solution.py:208
  80.8 6.6 %collective-permute-done.6 = bf16[2,64,1536]{2,1,0:T(8,128)(2,1)S(1)} collective-permute-done((bf16[2,64,1536]{2,1,0:T(8,128)(2,1)S(1)}, bf16[2,64,1536]{2,1,0:T(8,128)(2,1)S(1)}, u32[]{:S(2)}, u32[]{:S(2)}) %collective-permute-start.6) | collective-permute-done | bytes 393248 | tf_op jit(solution)/shard_map/ppermute | solution.py:204
  87.4 0.0 collective-permute-done.7
  87.4 3.0 %collective-permute-start.8 = (bf16[4,64,1536]{2,1,0:T(8,128)(2,1)S(1)}, bf16[4,64,1536]{2,1,0:T(8,128)(2,1)S(1)}, u32[]{:S(2)}, u32[]{:S(2)}) collective-permute-start(bf16[4,64,1536]{2,1,0:T(8,128)(2,1)S(1)} %constant_dynamic-update-slice_fusion.4.odd), channel_id=1, source_target_pairs={{0,32},{32,0},{1,33},{33,1},{2,34},{34,2},{3,35},{35,3},{4,36},{36... | collective-permute-start | bytes 2359304 | tf_op jit(solution)/shard_map/ppermute | solution.py:208
  90.5 1.9 %collective-permute-done.8.odd_core = bf16[4,64,1536]{2,1,0:T(8,128)(2,1)S(1)} collective-permute-done((bf16[4,64,1536]{2,1,0:T(8,128)(2,1)S(1)}, bf16[4,64,1536]{2,1,0:T(8,128)(2,1)S(1)}, u32[]{:S(2)}, u32[]{:S(2)}) %collective-permute-start.8) | collective-permute-done | bytes 786464 | tf_op jit(solution)/shard_map/ppermute | solution.py:208
  92.4 1.6 %shard_map.50 = (bf16[1024,1024]{1,0:T(8,128)(2,1)S(1)}, bf16[1024,512]{1,0:T(8,128)(2,1)S(1)}) custom-call(s32[64]{0:T(128)S(1)} %copy-done, bf16[4,64,1536]{2,1,0:T(8,128)(2,1)S(1)} %constant_dynamic-update-slice_fusion.near, bf16[4,64,1536]{2,1,0:T(8,128)(2,1)S(1)} %collective-permute-done.5.near_core, ...), custom_call_target="tpu_custom_call" | custom-call | flops 1073741824 | bytes 6291456 | tf_op jit(solution)/shard_map/pallas_call | solution.py:106
  94.0 1.3 %copy-done.1 = bf16[1024,1024]{1,0:T(8,128)(2,1)} copy-done((bf16[1024,1024]{1,0:T(8,128)(2,1)}, bf16[1024,1024]{1,0:T(8,128)(2,1)S(1)}, u32[]{:S(2)}) %copy-start.1) | copy-done | bytes 2097176
  95.3 1.0 copy-done.2
  96.3 7.1 %shard_map.51 = (bf16[4,32,256]{2,1,0:T(8,128)(2,1)}, bf16[4,2,256,256]{3,2,1,0:T(8,128)(2,1)}) custom-call(s32[64]{0:T(128)} %ranks.3, bf16[1024,1024]{1,0:T(8,128)(2,1)} %copy-done.1, bf16[1024,512]{1,0:T(8,128)(2,1)} %copy-done.2, bf16[32,4,32,256]{3,2,1,0:T(8,128)(2,1)} %all-to-all-done.1.full), custom_call_target="tpu_custom_call" | custom-call | flops 3221225472 | bytes 6291456 | tf_op jit(solution)/shard_map/pallas_call | solution.py:180
  (16 shorter events, 0.2 us)
Async XLA Ops:
  0.6 36.5 %copy-start.3 = (bf16[4,32,256]{2,1,0:T(8,128)(2,1)S(1)}, bf16[4,32,256]{2,1,0:T(8,128)(2,1)}, u32[]{:S(2)}) copy-start(bf16[4,32,256]{2,1,0:T(8,128)(2,1)} %param.3) | copy-start | bytes 196612
  1.5 26.1 %collective-permute-start = (bf16[2,32,256]{2,1,0:T(8,128)(2,1)S(1)}, bf16[2,32,256]{2,1,0:T(8,128)(2,1)S(1)}, u32[]{:S(2)}, u32[]{:S(2)}) collective-permute-start(bf16[2,32,256]{2,1,0:T(8,128)(2,1)S(1)} %get-tuple-element.16), channel_id=1, source_target_pairs={{0,0},{1,1},{2,32},{3,33},{4,64},{5,65},{6,96},{7,97},{8,128},{9,1... | collective-permute-start | bytes 98312 | tf_op jit(solution)/shard_map/ppermute | solution.py:43
  7.1 20.5 %collective-permute-start.1 = (bf16[2,32,256]{2,1,0:T(8,128)(2,1)S(1)}, bf16[2,32,256]{2,1,0:T(8,128)(2,1)S(1)}, u32[]{:S(2)}, u32[]{:S(2)}) collective-permute-start(bf16[2,32,256]{2,1,0:T(8,128)(2,1)S(1)} %get-tuple-element.17), channel_id=1, source_target_pairs={{0,1},{1,0},{2,33},{3,32},{4,65},{5,64},{6,97},{7,96},{8,129},{9,1... | collective-permute-start | bytes 98312 | tf_op jit(solution)/shard_map/ppermute | solution.py:43
  11.6 25.1 %all-to-all-start = ((bf16[32,2,1024]{2,1,0:T(2,128)(2,1)}), bf16[32,2,1024]{2,1,0:T(2,128)(2,1)S(1)}, u32[]{:S(2)}, u32[]{:S(2)}) async-start(bf16[32,2,1024]{2,1,0:T(2,128)(2,1)} %reshape.8), calls=%async_computation | async-start | bytes 262144 | tf_op jit(solution)/shard_map/all_to_all | solution.py:28
  38.7 57.6 %all-to-all-start.1 = ((bf16[32,4,32,256]{3,2,1,0:T(8,128)(2,1)}), bf16[32,4,32,256]{3,2,1,0:T(8,128)(2,1)}, u32[]{:S(2)}, u32[]{:S(2)}) async-start(bf16[32,4,32,256]{3,2,1,0:T(8,128)(2,1)} %broadcast_in_dim.9), calls=%async_computation.1 | async-start | bytes 4194304 | tf_op jit(solution)/shard_map/all_to_all | solution.py:28
  43.5 33.7 %collective-permute-start.4 = (bf16[1,64,1536]{2,1,0:T(8,128)(2,1)S(1)}, bf16[1,64,1536]{2,1,0:T(8,128)(2,1)S(1)}, u32[]{:S(2)}, u32[]{:S(2)}) collective-permute-start(bf16[1,64,1536]{2,1,0:T(8,128)(2,1)S(1)} %maximum_bitcast_fusion), channel_id=1, source_target_pairs={{256,0},{320,64},{384,128},{448,192},{0,256},{64,320},{128,384},{1... | collective-permute-start | bytes 589832 | tf_op jit(solution)/shard_map/ppermute | solution.py:204
  51.7 12.5 %collective-permute-start.3 = (bf16[1,64,1536]{2,1,0:T(8,128)(2,1)S(1)}, bf16[1,64,1536]{2,1,0:T(8,128)(2,1)S(1)}, u32[]{:S(2)}, u32[]{:S(2)}) collective-permute-start(bf16[1,64,1536]{2,1,0:T(8,128)(2,1)S(1)} %maximum_bitcast_fusion), channel_id=1, source_target_pairs={{384,0},{448,64},{0,128},{64,192},{128,256},{192,320},{256,384},{3... | collective-permute-start | bytes 589832 | tf_op jit(solution)/shard_map/ppermute | solution.py:204
  56.6 14.0 %collective-permute-start.2 = (bf16[1,64,1536]{2,1,0:T(8,128)(2,1)S(1)}, bf16[1,64,1536]{2,1,0:T(8,128)(2,1)S(1)}, u32[]{:S(2)}, u32[]{:S(2)}) collective-permute-start(bf16[1,64,1536]{2,1,0:T(8,128)(2,1)S(1)} %maximum_bitcast_fusion), channel_id=1, source_target_pairs={{128,0},{192,64},{256,128},{320,192},{384,256},{448,320},{0,384},{... | collective-permute-start | bytes 589832 | tf_op jit(solution)/shard_map/ppermute | solution.py:204
  59.1 33.3 %copy-start = (s32[64]{0:T(128)S(1)}, s32[64]{0:T(128)}, u32[]{:S(2)}) copy-start(s32[64]{0:T(128)} %ranks.3) | copy-start | bytes 772
  70.7 16.7 %collective-permute-start.7 = (bf16[2,64,1536]{2,1,0:T(8,128)(2,1)S(1)}, bf16[2,64,1536]{2,1,0:T(8,128)(2,1)S(1)}, u32[]{:S(2)}, u32[]{:S(2)}) collective-permute-start(bf16[2,64,1536]{2,1,0:T(8,128)(2,1)S(1)} %get-tuple-element.10), channel_id=1, source_target_pairs={{448,0},{0,64},{64,128},{128,192},{192,256},{256,320},{320,384},{3... | collective-permute-start | bytes 1179656 | tf_op jit(solution)/shard_map/ppermute | solution.py:204
  73.0 14.4 %collective-permute-start.6 = (bf16[2,64,1536]{2,1,0:T(8,128)(2,1)S(1)}, bf16[2,64,1536]{2,1,0:T(8,128)(2,1)S(1)}, u32[]{:S(2)}, u32[]{:S(2)}) collective-permute-start(bf16[2,64,1536]{2,1,0:T(8,128)(2,1)S(1)} %get-tuple-element.11), channel_id=1, source_target_pairs={{64,0},{128,64},{192,128},{256,192},{320,256},{384,320},{448,384},... | collective-permute-start | bytes 1179656 | tf_op jit(solution)/shard_map/ppermute | solution.py:204
  77.2 13.3 %collective-permute-start.5 = (bf16[4,64,1536]{2,1,0:T(8,128)(2,1)S(1)}, bf16[4,64,1536]{2,1,0:T(8,128)(2,1)S(1)}, u32[]{:S(2)}, u32[]{:S(2)}) collective-permute-start(bf16[4,64,1536]{2,1,0:T(8,128)(2,1)S(1)} %constant_dynamic-update-slice_fusion.near), channel_id=1, source_target_pairs={{0,32},{32,0},{1,33},{33,1},{2,34},{34,2},{3,35},{35,3},{4,36},{36... | collective-permute-start | bytes 2359304 | tf_op jit(solution)/shard_map/ppermute | solution.py:208
  87.4 4.9 %collective-permute-start.8 = (bf16[4,64,1536]{2,1,0:T(8,128)(2,1)S(1)}, bf16[4,64,1536]{2,1,0:T(8,128)(2,1)S(1)}, u32[]{:S(2)}, u32[]{:S(2)}) collective-permute-start(bf16[4,64,1536]{2,1,0:T(8,128)(2,1)S(1)} %constant_dynamic-update-slice_fusion.4.odd), channel_id=1, source_target_pairs={{0,32},{32,0},{1,33},{33,1},{2,34},{34,2},{3,35},{35,3},{4,36},{36... | collective-permute-start | bytes 2359304 | tf_op jit(solution)/shard_map/ppermute | solution.py:208
  94.0 1.3 %copy-start.1 = (bf16[1024,1024]{1,0:T(8,128)(2,1)}, bf16[1024,1024]{1,0:T(8,128)(2,1)S(1)}, u32[]{:S(2)}) copy-start(bf16[1024,1024]{1,0:T(8,128)(2,1)S(1)} %get-tuple-element.7.factor_in) | copy-start | bytes 6291460
  95.3 1.0 copy-start.2
where the time goes:
time: 104 us; the launch traced here: 103 us
  starting transfers between devices  57.9 us (56%)
  waiting for transfers between devices  29 us (28%)
  Pallas kernels  8.67 us (8%)
  local copies, waits for them, and re-layouts  6.76 us (6%)
    ppermute x5, starting transfers between devices, from_level(): lax.ppermute(value, 'z', [((z + shift) % levels, z) for z in range(levels)])  22.1 us
    all_to_all x2, starting transfers between devices, exchanged(): return lax.all_to_all(copies, axes, split_axis=0, concat_axis=0, tiled=True)  20.7 us
    ppermute x5, waiting for transfers between devices, from_level(): lax.ppermute(value, 'z', [((z + shift) % levels, z) for z in range(levels)])  18 us
    all_to_all x2, waiting for transfers between devices, exchanged(): return lax.all_to_all(copies, axes, split_axis=0, concat_axis=0, tiled=True)  9.11 us
    ppermute x2, starting transfers between devices, moved(): return lax.ppermute(part, ALL, pairs)  8.52 us
    pallas_call x1, Pallas kernels, solve_rows(): pl.pallas_call(row_kernel, out_shape=(jax.ShapeDtypeStruct((tiles, depth,...  7.07 us
    ppermute x2, starting transfers between devices, other_core(): return lax.ppermute(value, 'core', [(0, 1), (1, 0)])  6.6 us
    unnamed x14, local copies, waits for them, and re-layouts  3.43 us
  transfers between devices with their start and end apart: 11, of which 5 were waited for; matrix products, arithmetic and copies ran while one was open for 2% of the time, Pallas kernels for 2%

commit v1 on v0

--- a/solution.py
+++ b/solution.py
@@ -31,20 +31,15 @@
 def column_tiles(panel, col, rows, cols):
     odd = lax.rem(col, 2)
     pair = panel.shape[0] // 2
-
-    def moved(flip):
-        half = lax.bitwise_xor(odd, flip)
-        part = lax.dynamic_slice_in_dim(panel, pair * half, pair, 0)
-        pairs = [
-            (r * cols + c, (c // 2) * cols + 2 * r + ((c % 2) ^ flip))
-            for r in range(rows)
-            for c in range(cols)
-        ]
-        return lax.ppermute(part, ALL, pairs)
-
-    first, second = moved(0), moved(1)
-    low = jnp.where(odd == 0, first, second)
-    high = jnp.where(odd == 0, second, first)
+    moves = [
+        (r * cols + c, (c // 2) * cols + 2 * r + c % 2) for r in range(rows) for c in range(cols)
+    ]
+    moved = lax.ppermute(panel, ALL, moves)
+    kept = lax.dynamic_slice_in_dim(moved, pair * odd, pair, 0)
+    given = lax.dynamic_slice_in_dim(moved, pair * (1 - odd), pair, 0)
+    taken = lax.ppermute(given, "y", [(y, y ^ 1) for y in range(lax.axis_size("y"))])
+    low = jnp.where(odd == 0, kept, taken)
+    high = jnp.where(odd == 0, taken, kept)
     return jnp.concatenate([low, high], axis=1)
 
 
@@ -224,7 +219,9 @@
     copies = copies_for(panel, COL)
     copies, packed = lax.optimization_barrier((copies, packed))
     full = exchanged(copies, COL)
-    opposite, above, below = from_level(packed, 4), from_level(packed, 2), from_level(packed, 6)
+    above = from_level(packed, 2)
+    below = from_level(packed, 6)
+    opposite = from_level(packed, 4)
     near = jnp.concatenate([packed, above, below, opposite])
     upper, lower = jnp.concatenate([packed, above]), jnp.concatenate([packed, below])
     upper = from_level(upper, 1)

time: 104 us -> 105 us (level)
  starting transfers between devices: 57.9 us -> 60.8 us
    ppermute x5, waiting for transfers between devices: 18 us -> 15.2 us  [from_level(): lax.ppermute(value, 'z', [((z + shift) % levels, z) for z in range(levels)])]
    ppermute x2, waiting for transfers between devices: 0.01 us -> 2.14 us  [the longest x1 2.14 us: column_tiles(): moved = lax.ppermute(panel, ALL, moves)]
    all_to_all x2, starting transfers between devices: 20.7 us -> 22.2 us  [exchanged(): return lax.all_to_all(copies, axes, split_axis=0, concat_axis=0, tiled=True)]
  transfers between devices with their start and end apart: 11 -> 11, of which waited for: 5 -> 6; matrix products, arithmetic and copies ran while one was open for 2% -> 2% of each run, Pallas kernels for 2% -> 2%
where the time goes in v1:
time: 105 us
  starting transfers between devices  60.8 us (58%)
  waiting for transfers between devices  28.3 us (27%)
  Pallas kernels  8.67 us (8%)
  local copies, waits for them, and re-layouts  5.96 us (6%)
    all_to_all x2, starting transfers between devices, exchanged(): return lax.all_to_all(copies, axes, split_axis=0, concat_axis=0, tiled=True)  22.2 us
    ppermute x5, starting transfers between devices, from_level(): lax.ppermute(value, 'z', [((z + shift) % levels, z) for z in range(levels)])  22.1 us
    ppermute x5, waiting for transfers between devices, from_level(): lax.ppermute(value, 'z', [((z + shift) % levels, z) for z in range(levels)])  15.2 us
    all_to_all x2, waiting for transfers between devices, exchanged(): return lax.all_to_all(copies, axes, split_axis=0, concat_axis=0, tiled=True)  9.1 us
    ppermute x2, starting transfers between devices, other_core(): return lax.ppermute(value, 'core', [(0, 1), (1, 0)])  7.43 us
    pallas_call x1, Pallas kernels, solve_rows(): pl.pallas_call(row_kernel, out_shape=(jax.ShapeDtypeStruct((tiles, depth,...  7.07 us
    ppermute x1, starting transfers between devices, column_tiles(): moved = lax.ppermute(panel, ALL, moves)  5.73 us
    unnamed x14, local copies, waits for them, and re-layouts  3.43 us
  transfers between devices with their start and end apart: 11, of which 6 were waited for; matrix products, arithmetic and copies ran while one was open for 2% of the time, Pallas kernels for 2%

profile of v1, /device:TPU:1, one launch (start us, length us, event | category | flops | bytes accessed | tf_op | source)
XLA Modules:
  0.0 104.7 jit_solution(11321046439526259317)
XLA Ops:
  0.6 5.7 %collective-permute-start = (bf16[4,32,256]{2,1,0:T(8,128)(2,1)}, bf16[4,32,256]{2,1,0:T(8,128)(2,1)S(1)}, u32[]{:S(2)}, u32[]{:S(2)}) collective-permute-start(bf16[4,32,256]{2,1,0:T(8,128)(2,1)} %param.3), channel_id=1, source_target_pairs={{0,0},{1,1},{2,32},{3,33},{4,64},{5,65},{6,96},{7,97},{8,128},{9,1... | collective-permute-start | bytes 196616 | tf_op jit(solution)/shard_map/ppermute | solution.py:37
  6.4 2.1 %collective-permute-done = bf16[4,32,256]{2,1,0:T(8,128)(2,1)S(1)} collective-permute-done((bf16[4,32,256]{2,1,0:T(8,128)(2,1)}, bf16[4,32,256]{2,1,0:T(8,128)(2,1)S(1)}, u32[]{:S(2)}, u32[]{:S(2)}) %collective-permute-start) | collective-permute-done | bytes 65568 | tf_op jit(solution)/shard_map/ppermute | solution.py:37
  8.5 3.3 %collective-permute-start.1 = (bf16[2,32,256]{2,1,0:T(8,128)(2,1)S(1)}, bf16[2,32,256]{2,1,0:T(8,128)(2,1)S(1)}, u32[]{:S(2)}, u32[]{:S(2)}) collective-permute-start(bf16[2,32,256]{2,1,0:T(8,128)(2,1)S(1)} %constant_dynamic-slice_fusion), channel_id=1, source_target_pairs={{0,1},{1,0},{2,3},{3,2},{4,5},{5,4},{6,7},{7,6},{8,9},{9,8},{10,11... | collective-permute-start | bytes 98312 | tf_op jit(solution)/shard_map/ppermute | solution.py:40
  11.8 0.7 broadcast_in_dim.10
  12.6 0.8 reshape.8
  13.4 17.5 %all-to-all-start = ((bf16[32,2,1024]{2,1,0:T(2,128)(2,1)}), bf16[32,2,1024]{2,1,0:T(2,128)(2,1)S(1)}, u32[]{:S(2)}, u32[]{:S(2)}) async-start(bf16[32,2,1024]{2,1,0:T(2,128)(2,1)} %reshape.8), calls=%async_computation | async-start | bytes 262144 | tf_op jit(solution)/shard_map/all_to_all | solution.py:28
  30.9 0.0 collective-permute-done.1
  31.0 9.1 %all-to-all-done = bf16[32,2,1024]{2,1,0:T(2,128)(2,1)S(1)} async-done(((bf16[32,2,1024]{2,1,0:T(2,128)(2,1)}), bf16[32,2,1024]{2,1,0:T(2,128)(2,1)S(1)}, u32[]{:S(2)}, u32[]{:S(2)}) %all-to-all-start) | async-done | bytes 131104 | tf_op jit(solution)/shard_map/all_to_all | solution.py:28
  40.1 0.2 reshape.9
  40.3 0.1 copy.6
  40.5 1.6 %broadcast_in_dim.9 = bf16[32,4,32,256]{3,2,1,0:T(8,128)(2,1)} broadcast(bf16[4,32,256]{2,1,0:T(8,128)(2,1)S(1)} %copy-done.3), dimensions={1,2,3} | broadcast | bytes 2162688 | tf_op jit(solution)/shard_map/broadcast_in_dim | solution.py:24
  42.1 4.8 %all-to-all-start.1 = ((bf16[32,4,32,256]{3,2,1,0:T(8,128)(2,1)}), bf16[32,4,32,256]{3,2,1,0:T(8,128)(2,1)}, u32[]{:S(2)}, u32[]{:S(2)}) async-start(bf16[32,4,32,256]{3,2,1,0:T(8,128)(2,1)} %broadcast_in_dim.9), calls=%async_computation.1 | async-start | bytes 4194304 | tf_op jit(solution)/shard_map/all_to_all | solution.py:28
  46.8 8.2 %collective-permute-start.4 = (bf16[1,64,1536]{2,1,0:T(8,128)(2,1)S(1)}, bf16[1,64,1536]{2,1,0:T(8,128)(2,1)S(1)}, u32[]{:S(2)}, u32[]{:S(2)}) collective-permute-start(bf16[1,64,1536]{2,1,0:T(8,128)(2,1)S(1)} %maximum_bitcast_fusion), channel_id=1, source_target_pairs={{256,0},{320,64},{384,128},{448,192},{0,256},{64,320},{128,384},{1... | collective-permute-start | bytes 589832 | tf_op jit(solution)/shard_map/ppermute | solution.py:199
  55.1 4.8 %collective-permute-start.3 = (bf16[1,64,1536]{2,1,0:T(8,128)(2,1)S(1)}, bf16[1,64,1536]{2,1,0:T(8,128)(2,1)S(1)}, u32[]{:S(2)}, u32[]{:S(2)}) collective-permute-start(bf16[1,64,1536]{2,1,0:T(8,128)(2,1)S(1)} %maximum_bitcast_fusion), channel_id=1, source_target_pairs={{384,0},{448,64},{0,128},{64,192},{128,256},{192,320},{256,384},{3... | collective-permute-start | bytes 589832 | tf_op jit(solution)/shard_map/ppermute | solution.py:199
  59.9 2.6 %collective-permute-start.2 = (bf16[1,64,1536]{2,1,0:T(8,128)(2,1)S(1)}, bf16[1,64,1536]{2,1,0:T(8,128)(2,1)S(1)}, u32[]{:S(2)}, u32[]{:S(2)}) collective-permute-start(bf16[1,64,1536]{2,1,0:T(8,128)(2,1)S(1)} %maximum_bitcast_fusion), channel_id=1, source_target_pairs={{128,0},{192,64},{256,128},{320,192},{384,256},{448,320},{0,384},{... | collective-permute-start | bytes 589832 | tf_op jit(solution)/shard_map/ppermute | solution.py:199
  62.5 0.0 copy-start
  62.5 4.9 %collective-permute-done.3 = bf16[1,64,1536]{2,1,0:T(8,128)(2,1)S(1)} collective-permute-done((bf16[1,64,1536]{2,1,0:T(8,128)(2,1)S(1)}, bf16[1,64,1536]{2,1,0:T(8,128)(2,1)S(1)}, u32[]{:S(2)}, u32[]{:S(2)}) %collective-permute-start.3) | collective-permute-done | bytes 196640 | tf_op jit(solution)/shard_map/ppermute | solution.py:199
  67.4 6.6 %collective-permute-done.2 = bf16[1,64,1536]{2,1,0:T(8,128)(2,1)S(1)} collective-permute-done((bf16[1,64,1536]{2,1,0:T(8,128)(2,1)S(1)}, bf16[1,64,1536]{2,1,0:T(8,128)(2,1)S(1)}, u32[]{:S(2)}, u32[]{:S(2)}) %collective-permute-start.2) | collective-permute-done | bytes 196640 | tf_op jit(solution)/shard_map/ppermute | solution.py:199
  74.0 0.1 pad_maximum_fusion
  74.1 2.3 %collective-permute-start.7 = (bf16[2,64,1536]{2,1,0:T(8,128)(2,1)S(1)}, bf16[2,64,1536]{2,1,0:T(8,128)(2,1)S(1)}, u32[]{:S(2)}, u32[]{:S(2)}) collective-permute-start(bf16[2,64,1536]{2,1,0:T(8,128)(2,1)S(1)} %get-tuple-element.10), channel_id=1, source_target_pairs={{448,0},{0,64},{64,128},{128,192},{192,256},{256,320},{320,384},{3... | collective-permute-start | bytes 1179656 | tf_op jit(solution)/shard_map/ppermute | solution.py:199
  76.4 4.2 %collective-permute-start.6 = (bf16[2,64,1536]{2,1,0:T(8,128)(2,1)S(1)}, bf16[2,64,1536]{2,1,0:T(8,128)(2,1)S(1)}, u32[]{:S(2)}, u32[]{:S(2)}) collective-permute-start(bf16[2,64,1536]{2,1,0:T(8,128)(2,1)S(1)} %get-tuple-element.11), channel_id=1, source_target_pairs={{64,0},{128,64},{192,128},{256,192},{320,256},{384,320},{448,384},... | collective-permute-start | bytes 1179656 | tf_op jit(solution)/shard_map/ppermute | solution.py:199
  80.6 0.0 collective-permute-done.4
  80.6 3.8 %collective-permute-start.5 = (bf16[4,64,1536]{2,1,0:T(8,128)(2,1)S(1)}, bf16[4,64,1536]{2,1,0:T(8,128)(2,1)S(1)}, u32[]{:S(2)}, u32[]{:S(2)}) collective-permute-start(bf16[4,64,1536]{2,1,0:T(8,128)(2,1)S(1)} %constant_dynamic-update-slice_fusion.near), channel_id=1, source_target_pairs={{0,32},{32,0},{1,33},{33,1},{2,34},{34,2},{3,35},{35,3},{4,36},{36... | collective-permute-start | bytes 2359304 | tf_op jit(solution)/shard_map/ppermute | solution.py:203
  84.4 3.7 %collective-permute-done.6 = bf16[2,64,1536]{2,1,0:T(8,128)(2,1)S(1)} collective-permute-done((bf16[2,64,1536]{2,1,0:T(8,128)(2,1)S(1)}, bf16[2,64,1536]{2,1,0:T(8,128)(2,1)S(1)}, u32[]{:S(2)}, u32[]{:S(2)}) %collective-permute-start.6) | collective-permute-done | bytes 393248 | tf_op jit(solution)/shard_map/ppermute | solution.py:199
  88.2 0.0 collective-permute-done.7
  88.2 3.7 %collective-permute-start.8 = (bf16[4,64,1536]{2,1,0:T(8,128)(2,1)S(1)}, bf16[4,64,1536]{2,1,0:T(8,128)(2,1)S(1)}, u32[]{:S(2)}, u32[]{:S(2)}) collective-permute-start(bf16[4,64,1536]{2,1,0:T(8,128)(2,1)S(1)} %constant_dynamic-update-slice_fusion.4.odd), channel_id=1, source_target_pairs={{0,32},{32,0},{1,33},{33,1},{2,34},{34,2},{3,35},{35,3},{4,36},{36... | collective-permute-start | bytes 2359304 | tf_op jit(solution)/shard_map/ppermute | solution.py:203
  91.9 1.9 %collective-permute-done.8.odd_core = bf16[4,64,1536]{2,1,0:T(8,128)(2,1)S(1)} collective-permute-done((bf16[4,64,1536]{2,1,0:T(8,128)(2,1)S(1)}, bf16[4,64,1536]{2,1,0:T(8,128)(2,1)S(1)}, u32[]{:S(2)}, u32[]{:S(2)}) %collective-permute-start.8) | collective-permute-done | bytes 786464 | tf_op jit(solution)/shard_map/ppermute | solution.py:203
  93.8 1.6 %shard_map.50 = (bf16[1024,1024]{1,0:T(8,128)(2,1)S(1)}, bf16[1024,512]{1,0:T(8,128)(2,1)S(1)}) custom-call(s32[64]{0:T(128)S(1)} %copy-done, bf16[4,64,1536]{2,1,0:T(8,128)(2,1)S(1)} %constant_dynamic-update-slice_fusion.near, bf16[4,64,1536]{2,1,0:T(8,128)(2,1)S(1)} %collective-permute-done.5.near_core, ...), custom_call_target="tpu_custom_call" | custom-call | flops 1073741824 | bytes 6291456 | tf_op jit(solution)/shard_map/pallas_call | solution.py:101
  95.4 1.3 %copy-done.1 = bf16[1024,1024]{1,0:T(8,128)(2,1)} copy-done((bf16[1024,1024]{1,0:T(8,128)(2,1)}, bf16[1024,1024]{1,0:T(8,128)(2,1)S(1)}, u32[]{:S(2)}) %copy-start.1) | copy-done | bytes 2097176
  96.7 1.0 copy-done.2
  97.6 0.0 all-to-all-done.1.full
  97.7 7.1 %shard_map.51 = (bf16[4,32,256]{2,1,0:T(8,128)(2,1)}, bf16[4,2,256,256]{3,2,1,0:T(8,128)(2,1)}) custom-call(s32[64]{0:T(128)} %ranks.3, bf16[1024,1024]{1,0:T(8,128)(2,1)} %copy-done.1, bf16[1024,512]{1,0:T(8,128)(2,1)} %copy-done.2, bf16[32,4,32,256]{3,2,1,0:T(8,128)(2,1)} %all-to-all-done.1.full), custom_call_target="tpu_custom_call" | custom-call | flops 3221225472 | bytes 6291456 | tf_op jit(solution)/shard_map/pallas_call | solution.py:175
  (16 shorter events, 0.2 us)
Async XLA Ops:
  0.6 39.8 %copy-start.3 = (bf16[4,32,256]{2,1,0:T(8,128)(2,1)S(1)}, bf16[4,32,256]{2,1,0:T(8,128)(2,1)}, u32[]{:S(2)}) copy-start(bf16[4,32,256]{2,1,0:T(8,128)(2,1)} %param.3) | copy-start | bytes 196612
  0.6 7.9 %collective-permute-start = (bf16[4,32,256]{2,1,0:T(8,128)(2,1)}, bf16[4,32,256]{2,1,0:T(8,128)(2,1)S(1)}, u32[]{:S(2)}, u32[]{:S(2)}) collective-permute-start(bf16[4,32,256]{2,1,0:T(8,128)(2,1)} %param.3), channel_id=1, source_target_pairs={{0,0},{1,1},{2,32},{3,33},{4,64},{5,65},{6,96},{7,97},{8,128},{9,1... | collective-permute-start | bytes 196616 | tf_op jit(solution)/shard_map/ppermute | solution.py:37
  8.5 22.4 %collective-permute-start.1 = (bf16[2,32,256]{2,1,0:T(8,128)(2,1)S(1)}, bf16[2,32,256]{2,1,0:T(8,128)(2,1)S(1)}, u32[]{:S(2)}, u32[]{:S(2)}) collective-permute-start(bf16[2,32,256]{2,1,0:T(8,128)(2,1)S(1)} %constant_dynamic-slice_fusion), channel_id=1, source_target_pairs={{0,1},{1,0},{2,3},{3,2},{4,5},{5,4},{6,7},{7,6},{8,9},{9,8},{10,11... | collective-permute-start | bytes 98312 | tf_op jit(solution)/shard_map/ppermute | solution.py:40
  13.4 26.6 %all-to-all-start = ((bf16[32,2,1024]{2,1,0:T(2,128)(2,1)}), bf16[32,2,1024]{2,1,0:T(2,128)(2,1)S(1)}, u32[]{:S(2)}, u32[]{:S(2)}) async-start(bf16[32,2,1024]{2,1,0:T(2,128)(2,1)} %reshape.8), calls=%async_computation | async-start | bytes 262144 | tf_op jit(solution)/shard_map/all_to_all | solution.py:28
  42.1 55.6 %all-to-all-start.1 = ((bf16[32,4,32,256]{3,2,1,0:T(8,128)(2,1)}), bf16[32,4,32,256]{3,2,1,0:T(8,128)(2,1)}, u32[]{:S(2)}, u32[]{:S(2)}) async-start(bf16[32,4,32,256]{3,2,1,0:T(8,128)(2,1)} %broadcast_in_dim.9), calls=%async_computation.1 | async-start | bytes 4194304 | tf_op jit(solution)/shard_map/all_to_all | solution.py:28
  46.8 33.8 %collective-permute-start.4 = (bf16[1,64,1536]{2,1,0:T(8,128)(2,1)S(1)}, bf16[1,64,1536]{2,1,0:T(8,128)(2,1)S(1)}, u32[]{:S(2)}, u32[]{:S(2)}) collective-permute-start(bf16[1,64,1536]{2,1,0:T(8,128)(2,1)S(1)} %maximum_bitcast_fusion), channel_id=1, source_target_pairs={{256,0},{320,64},{384,128},{448,192},{0,256},{64,320},{128,384},{1... | collective-permute-start | bytes 589832 | tf_op jit(solution)/shard_map/ppermute | solution.py:199
  55.1 12.4 %collective-permute-start.3 = (bf16[1,64,1536]{2,1,0:T(8,128)(2,1)S(1)}, bf16[1,64,1536]{2,1,0:T(8,128)(2,1)S(1)}, u32[]{:S(2)}, u32[]{:S(2)}) collective-permute-start(bf16[1,64,1536]{2,1,0:T(8,128)(2,1)S(1)} %maximum_bitcast_fusion), channel_id=1, source_target_pairs={{384,0},{448,64},{0,128},{64,192},{128,256},{192,320},{256,384},{3... | collective-permute-start | bytes 589832 | tf_op jit(solution)/shard_map/ppermute | solution.py:199
  59.9 14.1 %collective-permute-start.2 = (bf16[1,64,1536]{2,1,0:T(8,128)(2,1)S(1)}, bf16[1,64,1536]{2,1,0:T(8,128)(2,1)S(1)}, u32[]{:S(2)}, u32[]{:S(2)}) collective-permute-start(bf16[1,64,1536]{2,1,0:T(8,128)(2,1)S(1)} %maximum_bitcast_fusion), channel_id=1, source_target_pairs={{128,0},{192,64},{256,128},{320,192},{384,256},{448,320},{0,384},{... | collective-permute-start | bytes 589832 | tf_op jit(solution)/shard_map/ppermute | solution.py:199
  62.5 31.3 %copy-start = (s32[64]{0:T(128)S(1)}, s32[64]{0:T(128)}, u32[]{:S(2)}) copy-start(s32[64]{0:T(128)} %ranks.3) | copy-start | bytes 772
  74.1 14.1 %collective-permute-start.7 = (bf16[2,64,1536]{2,1,0:T(8,128)(2,1)S(1)}, bf16[2,64,1536]{2,1,0:T(8,128)(2,1)S(1)}, u32[]{:S(2)}, u32[]{:S(2)}) collective-permute-start(bf16[2,64,1536]{2,1,0:T(8,128)(2,1)S(1)} %get-tuple-element.10), channel_id=1, source_target_pairs={{448,0},{0,64},{64,128},{128,192},{192,256},{256,320},{320,384},{3... | collective-permute-start | bytes 1179656 | tf_op jit(solution)/shard_map/ppermute | solution.py:199
  76.4 11.8 %collective-permute-start.6 = (bf16[2,64,1536]{2,1,0:T(8,128)(2,1)S(1)}, bf16[2,64,1536]{2,1,0:T(8,128)(2,1)S(1)}, u32[]{:S(2)}, u32[]{:S(2)}) collective-permute-start(bf16[2,64,1536]{2,1,0:T(8,128)(2,1)S(1)} %get-tuple-element.11), channel_id=1, source_target_pairs={{64,0},{128,64},{192,128},{256,192},{320,256},{384,320},{448,384},... | collective-permute-start | bytes 1179656 | tf_op jit(solution)/shard_map/ppermute | solution.py:199
  80.6 11.2 %collective-permute-start.5 = (bf16[4,64,1536]{2,1,0:T(8,128)(2,1)S(1)}, bf16[4,64,1536]{2,1,0:T(8,128)(2,1)S(1)}, u32[]{:S(2)}, u32[]{:S(2)}) collective-permute-start(bf16[4,64,1536]{2,1,0:T(8,128)(2,1)S(1)} %constant_dynamic-update-slice_fusion.near), channel_id=1, source_target_pairs={{0,32},{32,0},{1,33},{33,1},{2,34},{34,2},{3,35},{35,3},{4,36},{36... | collective-permute-start | bytes 2359304 | tf_op jit(solution)/shard_map/ppermute | solution.py:203
  88.2 5.6 %collective-permute-start.8 = (bf16[4,64,1536]{2,1,0:T(8,128)(2,1)S(1)}, bf16[4,64,1536]{2,1,0:T(8,128)(2,1)S(1)}, u32[]{:S(2)}, u32[]{:S(2)}) collective-permute-start(bf16[4,64,1536]{2,1,0:T(8,128)(2,1)S(1)} %constant_dynamic-update-slice_fusion.4.odd), channel_id=1, source_target_pairs={{0,32},{32,0},{1,33},{33,1},{2,34},{34,2},{3,35},{35,3},{4,36},{36... | collective-permute-start | bytes 2359304 | tf_op jit(solution)/shard_map/ppermute | solution.py:203
  95.4 1.3 %copy-start.1 = (bf16[1024,1024]{1,0:T(8,128)(2,1)}, bf16[1024,1024]{1,0:T(8,128)(2,1)S(1)}, u32[]{:S(2)}) copy-start(bf16[1024,1024]{1,0:T(8,128)(2,1)S(1)} %get-tuple-element.7.factor_in) | copy-start | bytes 6291460
  96.7 1.0 copy-start.2

commit v2 on v1

--- a/solution.py
+++ b/solution.py
@@ -115,7 +115,7 @@
 
 
 def row_kernel(
-    ranks, factor_in, others_in, full, shares, core_blocks, factor, others, values, solved, sems
+    ranks, factor_in, others_in, full, shares, blocks_out, factor, others, values, solved, blocks, sems
 ):
     _, tiles, depth, width = full.shape
     order, across = others.shape
@@ -131,6 +131,10 @@
         return pltpu.make_async_copy(full.at[:, t], values.at[t], sems.at[steps + t])
 
     all_others = pltpu.make_async_copy(others_in, others, sems.at[steps + tiles])
+
+    def tile_blocks(t):
+        sem = sems.at[steps + tiles + 1 + t]
+        return pltpu.make_async_copy(blocks.at[t], blocks_out.at[t], sem)
 
     tile_values(0).start()
     for i in range(steps):
@@ -159,7 +163,8 @@
             preferred_element_type=jnp.float32,
         ).astype(jnp.bfloat16)
         for u in range(across // width):
-            core_blocks[t, u] = paired[:, width * u : width * (u + 1)]
+            blocks[t, u] = paired[:, width * u : width * (u + 1)]
+        tile_blocks(t).start()
 
     def later(t, carry):
         one(t, False)
@@ -167,6 +172,8 @@
 
     one(0, True)
     lax.fori_loop(1, tiles, later, 0)
+    for t in range(tiles):
+        tile_blocks(t).wait()
 
 
 def solve_rows(ranks, factor, others, full):
@@ -179,13 +186,14 @@
             jax.ShapeDtypeStruct((tiles, across // width, width, width), jnp.bfloat16),
         ),
         in_specs=[IN_SMEM, IN_PLACE, IN_PLACE, IN_PLACE],
-        out_specs=(IN_VMEM, IN_VMEM),
+        out_specs=(IN_VMEM, IN_PLACE),
         scratch_shapes=[
             pltpu.VMEM((order, order), jnp.bfloat16),
             pltpu.VMEM((order, across), jnp.bfloat16),
             pltpu.VMEM((tiles, cols, depth, width), jnp.bfloat16),
             pltpu.VMEM((order, width), jnp.bfloat16),
-            pltpu.SemaphoreType.DMA((order // STEP + tiles + 1,)),
+            pltpu.VMEM((tiles, across // width, width, width), jnp.bfloat16),
+            pltpu.SemaphoreType.DMA((order // STEP + 2 * tiles + 1,)),
         ],
         compiler_params=WHOLE_VMEM,
         cost_estimate=pl.CostEstimate(
@@ -213,11 +221,9 @@
     part = column_tiles(panel, col, rows, cols)
     factor = copies_for(inverse_factor.T, COL)
     factor = exchanged(factor, COL)
-    factor = factor.reshape(order, -1).T
-    packed = jnp.concatenate([factor, *part], axis=1)[None]
-
     copies = copies_for(panel, COL)
-    copies, packed = lax.optimization_barrier((copies, packed))
+    copies, factor = lax.optimization_barrier((copies, factor))
+    packed = jnp.concatenate([factor.reshape(order, -1).T, *part], axis=1)[None]
     full = exchanged(copies, COL)
     above = from_level(packed, 2)
     below = from_level(packed, 6)

time: 105 us -> 145 us (1.38)
  the two profiles are of different devices: /device:TPU:1 before, /device:TPU:47 now
where the time goes in v2:
time: 145 us
  waiting for transfers between devices  67 us (46%)
  starting transfers between devices  48.2 us (33%)
  blocking collectives  13.3 us (9%)
  Pallas kernels  9.07 us (6%)
  local copies, waits for them, and re-layouts  6.1 us (4%)
    ppermute x1, waiting for transfers between devices, column_tiles(): moved = lax.ppermute(panel, ALL, moves)  45.9 us
    ppermute x5, starting transfers between devices, from_level(): lax.ppermute(value, 'z', [((z + shift) % levels, z) for z in range(levels)])  16.2 us
    ppermute x5, waiting for transfers between devices, from_level(): lax.ppermute(value, 'z', [((z + shift) % levels, z) for z in range(levels)])  16.1 us
    ppermute x1, starting transfers between devices, column_tiles(): moved = lax.ppermute(panel, ALL, moves)  13.6 us
    all_to_all x1, blocking collectives, exchanged(): return lax.all_to_all(copies, axes, split_axis=0, concat_axis=0, tiled=True)  13.3 us
    all_to_all x1, starting transfers between devices, exchanged(): return lax.all_to_all(copies, axes, split_axis=0, concat_axis=0, tiled=True)  9.67 us
    pallas_call x1, Pallas kernels, solve_rows(): pl.pallas_call(row_kernel, out_shape=(jax.ShapeDtypeStruct((tiles, depth,...  7.47 us
    ppermute x2, starting transfers between devices, other_core(): return lax.ppermute(value, 'core', [(0, 1), (1, 0)])  6.76 us
  transfers between devices with their start and end apart: 10, of which 6 were waited for; matrix products, arithmetic and copies ran while one was open for 0% of the time, Pallas kernels for 1%

profile of v2, /device:TPU:47, one launch (start us, length us, event | category | flops | bytes accessed | tf_op | source)
XLA Modules:
  0.0 144.7 jit_solution(17458726802238132556)
XLA Ops:
  0.6 0.7 broadcast_in_dim.10
  1.4 0.2 reshape.8
  1.6 13.3 %all_to_all.10 = bf16[32,2,1024]{2,1,0:T(2,128)(2,1)S(1)} all-to-all(bf16[32,2,1024]{2,1,0:T(2,128)(2,1)S(1)} %reshape.8), channel_id=1, replica_groups=mesh['z'=8,'core'=2,'x'=4,'y'=8] {'x','y'}, dimensions={0} | all-to-all | bytes 262144 | tf_op jit(solution)/shard_map/all_to_all | solution.py:28
  14.8 0.2 reshape.9
  15.0 2.5 %broadcast_in_dim.9 = bf16[32,4,32,256]{3,2,1,0:T(8,128)(2,1)} broadcast(bf16[4,32,256]{2,1,0:T(8,128)(2,1)} %param.3), dimensions={1,2,3} | broadcast | bytes 2162688 | tf_op jit(solution)/shard_map/broadcast_in_dim | solution.py:24
  17.5 9.7 %all-to-all-start.1 = ((bf16[32,4,32,256]{3,2,1,0:T(8,128)(2,1)}), bf16[32,4,32,256]{3,2,1,0:T(8,128)(2,1)}, u32[]{:S(2)}, u32[]{:S(2)}) async-start(bf16[32,4,32,256]{3,2,1,0:T(8,128)(2,1)} %broadcast_in_dim.9), calls=%async_computation.1 | async-start | bytes 4194304 | tf_op jit(solution)/shard_map/all_to_all | solution.py:28
  27.2 13.6 %collective-permute-start = (bf16[4,32,256]{2,1,0:T(8,128)(2,1)S(1)}, bf16[4,32,256]{2,1,0:T(8,128)(2,1)S(1)}, u32[]{:S(2)}, u32[]{:S(2)}) collective-permute-start(bf16[4,32,256]{2,1,0:T(8,128)(2,1)S(1)} %copy-done.3), channel_id=1, source_target_pairs={{0,0},{1,1},{2,32},{3,33},{4,64},{5,65},{6,96},{7,97},{8,128},{9,1... | collective-permute-start | bytes 196616 | tf_op jit(solution)/shard_map/ppermute | solution.py:37
  40.9 45.9 %collective-permute-done = bf16[4,32,256]{2,1,0:T(8,128)(2,1)S(1)} collective-permute-done((bf16[4,32,256]{2,1,0:T(8,128)(2,1)S(1)}, bf16[4,32,256]{2,1,0:T(8,128)(2,1)S(1)}, u32[]{:S(2)}, u32[]{:S(2)}) %collective-permute-start) | collective-permute-done | bytes 65568 | tf_op jit(solution)/shard_map/ppermute | solution.py:37
  86.7 1.9 %collective-permute-start.1 = (bf16[2,32,256]{2,1,0:T(8,128)(2,1)S(1)}, bf16[2,32,256]{2,1,0:T(8,128)(2,1)S(1)}, u32[]{:S(2)}, u32[]{:S(2)}) collective-permute-start(bf16[2,32,256]{2,1,0:T(8,128)(2,1)S(1)} %constant_dynamic-slice_fusion), channel_id=1, source_target_pairs={{0,1},{1,0},{2,3},{3,2},{4,5},{5,4},{6,7},{7,6},{8,9},{9,8},{10,11... | collective-permute-start | bytes 98312 | tf_op jit(solution)/shard_map/ppermute | solution.py:40
  88.6 3.2 %collective-permute-done.1 = bf16[2,32,256]{2,1,0:T(8,128)(2,1)S(1)} collective-permute-done((bf16[2,32,256]{2,1,0:T(8,128)(2,1)S(1)}, bf16[2,32,256]{2,1,0:T(8,128)(2,1)S(1)}, u32[]{:S(2)}, u32[]{:S(2)}) %collective-permute-start.1) | collective-permute-done | bytes 32800 | tf_op jit(solution)/shard_map/ppermute | solution.py:40
  91.9 0.1 copy.6
  92.0 0.0 copy-start
  92.1 3.2 %collective-permute-start.3 = (bf16[1,64,1536]{2,1,0:T(8,128)(2,1)S(1)}, bf16[1,64,1536]{2,1,0:T(8,128)(2,1)S(1)}, u32[]{:S(2)}, u32[]{:S(2)}) collective-permute-start(bf16[1,64,1536]{2,1,0:T(8,128)(2,1)S(1)} %maximum_bitcast_fusion), channel_id=1, source_target_pairs={{384,0},{448,64},{0,128},{64,192},{128,256},{192,320},{256,384},{3... | collective-permute-start | bytes 589832 | tf_op jit(solution)/shard_map/ppermute | solution.py:207
  95.3 4.2 %collective-permute-start.2 = (bf16[1,64,1536]{2,1,0:T(8,128)(2,1)S(1)}, bf16[1,64,1536]{2,1,0:T(8,128)(2,1)S(1)}, u32[]{:S(2)}, u32[]{:S(2)}) collective-permute-start(bf16[1,64,1536]{2,1,0:T(8,128)(2,1)S(1)} %maximum_bitcast_fusion), channel_id=1, source_target_pairs={{128,0},{192,64},{256,128},{320,192},{384,256},{448,320},{0,384},{... | collective-permute-start | bytes 589832 | tf_op jit(solution)/shard_map/ppermute | solution.py:207
  99.5 3.5 %collective-permute-start.4 = (bf16[1,64,1536]{2,1,0:T(8,128)(2,1)S(1)}, bf16[1,64,1536]{2,1,0:T(8,128)(2,1)S(1)}, u32[]{:S(2)}, u32[]{:S(2)}) collective-permute-start(bf16[1,64,1536]{2,1,0:T(8,128)(2,1)S(1)} %maximum_bitcast_fusion), channel_id=1, source_target_pairs={{256,0},{320,64},{384,128},{448,192},{0,256},{64,320},{128,384},{1... | collective-permute-start | bytes 589832 | tf_op jit(solution)/shard_map/ppermute | solution.py:207
  103.0 0.0 collective-permute-done.3
  103.0 8.9 %collective-permute-done.2 = bf16[1,64,1536]{2,1,0:T(8,128)(2,1)S(1)} collective-permute-done((bf16[1,64,1536]{2,1,0:T(8,128)(2,1)S(1)}, bf16[1,64,1536]{2,1,0:T(8,128)(2,1)S(1)}, u32[]{:S(2)}, u32[]{:S(2)}) %collective-permute-start.2) | collective-permute-done | bytes 196640 | tf_op jit(solution)/shard_map/ppermute | solution.py:207
  111.9 0.1 pad_maximum_fusion.1
  112.0 1.9 %collective-permute-start.6 = (bf16[2,64,1536]{2,1,0:T(8,128)(2,1)S(1)}, bf16[2,64,1536]{2,1,0:T(8,128)(2,1)S(1)}, u32[]{:S(2)}, u32[]{:S(2)}) collective-permute-start(bf16[2,64,1536]{2,1,0:T(8,128)(2,1)S(1)} %get-tuple-element.11), channel_id=1, source_target_pairs={{64,0},{128,64},{192,128},{256,192},{320,256},{384,320},{448,384},... | collective-permute-start | bytes 1179656 | tf_op jit(solution)/shard_map/ppermute | solution.py:207
  113.9 3.4 %collective-permute-start.7 = (bf16[2,64,1536]{2,1,0:T(8,128)(2,1)S(1)}, bf16[2,64,1536]{2,1,0:T(8,128)(2,1)S(1)}, u32[]{:S(2)}, u32[]{:S(2)}) collective-permute-start(bf16[2,64,1536]{2,1,0:T(8,128)(2,1)S(1)} %get-tuple-element.10), channel_id=1, source_target_pairs={{448,0},{0,64},{64,128},{128,192},{192,256},{256,320},{320,384},{3... | collective-permute-start | bytes 1179656 | tf_op jit(solution)/shard_map/ppermute | solution.py:207
  117.3 0.0 collective-permute-done.4
  117.3 0.1 pad_maximum_fusion.near
  117.4 3.0 %collective-permute-start.5 = (bf16[4,64,1536]{2,1,0:T(8,128)(2,1)S(1)}, bf16[4,64,1536]{2,1,0:T(8,128)(2,1)S(1)}, u32[]{:S(2)}, u32[]{:S(2)}) collective-permute-start(bf16[4,64,1536]{2,1,0:T(8,128)(2,1)S(1)} %pad_maximum_fusion.near), channel_id=1, source_target_pairs={{0,32},{32,0},{1,33},{33,1},{2,34},{34,2},{3,35},{35,3},{4,36},{36... | collective-permute-start | bytes 2359304 | tf_op jit(solution)/shard_map/ppermute | solution.py:211
  120.4 3.6 %collective-permute-done.6 = bf16[2,64,1536]{2,1,0:T(8,128)(2,1)S(1)} collective-permute-done((bf16[2,64,1536]{2,1,0:T(8,128)(2,1)S(1)}, bf16[2,64,1536]{2,1,0:T(8,128)(2,1)S(1)}, u32[]{:S(2)}, u32[]{:S(2)}) %collective-permute-start.6) | collective-permute-done | bytes 393248 | tf_op jit(solution)/shard_map/ppermute | solution.py:207
  124.1 3.5 %collective-permute-done.7 = bf16[2,64,1536]{2,1,0:T(8,128)(2,1)S(1)} collective-permute-done((bf16[2,64,1536]{2,1,0:T(8,128)(2,1)S(1)}, bf16[2,64,1536]{2,1,0:T(8,128)(2,1)S(1)}, u32[]{:S(2)}, u32[]{:S(2)}) %collective-permute-start.7) | collective-permute-done | bytes 393248 | tf_op jit(solution)/shard_map/ppermute | solution.py:207
  127.6 3.8 %collective-permute-start.8 = (bf16[4,64,1536]{2,1,0:T(8,128)(2,1)S(1)}, bf16[4,64,1536]{2,1,0:T(8,128)(2,1)S(1)}, u32[]{:S(2)}, u32[]{:S(2)}) collective-permute-start(bf16[4,64,1536]{2,1,0:T(8,128)(2,1)S(1)} %constant_dynamic-update-slice_fusion.odd), channel_id=1, source_target_pairs={{0,32},{32,0},{1,33},{33,1},{2,34},{34,2},{3,35},{35,3},{4,36},{36... | collective-permute-start | bytes 2359304 | tf_op jit(solution)/shard_map/ppermute | solution.py:211
  131.4 0.0 collective-permute-done.5.near_core
  131.4 1.9 %collective-permute-done.8.odd_core = bf16[4,64,1536]{2,1,0:T(8,128)(2,1)S(1)} collective-permute-done((bf16[4,64,1536]{2,1,0:T(8,128)(2,1)S(1)}, bf16[4,64,1536]{2,1,0:T(8,128)(2,1)S(1)}, u32[]{:S(2)}, u32[]{:S(2)}) %collective-permute-start.8) | collective-permute-done | bytes 786464 | tf_op jit(solution)/shard_map/ppermute | solution.py:211
  133.3 1.6 %shard_map.50 = (bf16[1024,1024]{1,0:T(8,128)(2,1)S(1)}, bf16[1024,512]{1,0:T(8,128)(2,1)S(1)}) custom-call(s32[64]{0:T(128)S(1)} %copy-done, bf16[4,64,1536]{2,1,0:T(8,128)(2,1)S(1)} %pad_maximum_fusion.near, bf16[4,64,1536]{2,1,0:T(8,128)(2,1)S(1)} %collective-permute-done.5.near_core, bf16[4,64,1536]{2,1,0:T(8,128)(2,1)S(1)} %constant_dynamic-update-slice_fusion.odd, ...), custom_call_target="tpu_custom_call" | custom-call | flops 1073741824 | bytes 6291456 | tf_op jit(solution)/shard_map/pallas_call | solution.py:101
  134.9 1.3 copy-done.1
  136.2 1.0 copy-done.2
  137.2 7.5 %shard_map.51 = (bf16[4,32,256]{2,1,0:T(8,128)(2,1)}, bf16[4,2,256,256]{3,2,1,0:T(8,128)(2,1)}) custom-call(s32[64]{0:T(128)} %ranks.3, bf16[1024,1024]{1,0:T(8,128)(2,1)} %copy-done.1, bf16[1024,512]{1,0:T(8,128)(2,1)} %copy-done.2, bf16[32,4,32,256]{3,2,1,0:T(8,128)(2,1)} %all-to-all-done.1.full), custom_call_target="tpu_custom_call" | custom-call | flops 3221225472 | bytes 6291456 | tf_op jit(solution)/shard_map/pallas_call | solution.py:182
  (12 shorter events, 0.1 us)
Async XLA Ops:
  17.5 9.7 %copy-start.3 = (bf16[4,32,256]{2,1,0:T(8,128)(2,1)S(1)}, bf16[4,32,256]{2,1,0:T(8,128)(2,1)}, u32[]{:S(2)}) copy-start(bf16[4,32,256]{2,1,0:T(8,128)(2,1)} %param.3) | copy-start | bytes 196612
  17.5 119.7 %all-to-all-start.1 = ((bf16[32,4,32,256]{3,2,1,0:T(8,128)(2,1)}), bf16[32,4,32,256]{3,2,1,0:T(8,128)(2,1)}, u32[]{:S(2)}, u32[]{:S(2)}) async-start(bf16[32,4,32,256]{3,2,1,0:T(8,128)(2,1)} %broadcast_in_dim.9), calls=%async_computation.1 | async-start | bytes 4194304 | tf_op jit(solution)/shard_map/all_to_all | solution.py:28
  27.2 59.5 %collective-permute-start = (bf16[4,32,256]{2,1,0:T(8,128)(2,1)S(1)}, bf16[4,32,256]{2,1,0:T(8,128)(2,1)S(1)}, u32[]{:S(2)}, u32[]{:S(2)}) collective-permute-start(bf16[4,32,256]{2,1,0:T(8,128)(2,1)S(1)} %copy-done.3), channel_id=1, source_target_pairs={{0,0},{1,1},{2,32},{3,33},{4,64},{5,65},{6,96},{7,97},{8,128},{9,1... | collective-permute-start | bytes 196616 | tf_op jit(solution)/shard_map/ppermute | solution.py:37
  86.7 5.2 %collective-permute-start.1 = (bf16[2,32,256]{2,1,0:T(8,128)(2,1)S(1)}, bf16[2,32,256]{2,1,0:T(8,128)(2,1)S(1)}, u32[]{:S(2)}, u32[]{:S(2)}) collective-permute-start(bf16[2,32,256]{2,1,0:T(8,128)(2,1)S(1)} %constant_dynamic-slice_fusion), channel_id=1, source_target_pairs={{0,1},{1,0},{2,3},{3,2},{4,5},{5,4},{6,7},{7,6},{8,9},{9,8},{10,11... | collective-permute-start | bytes 98312 | tf_op jit(solution)/shard_map/ppermute | solution.py:40
  92.0 41.3 %copy-start = (s32[64]{0:T(128)S(1)}, s32[64]{0:T(128)}, u32[]{:S(2)}) copy-start(s32[64]{0:T(128)} %ranks.3) | copy-start | bytes 772
  92.1 10.9 %collective-permute-start.3 = (bf16[1,64,1536]{2,1,0:T(8,128)(2,1)S(1)}, bf16[1,64,1536]{2,1,0:T(8,128)(2,1)S(1)}, u32[]{:S(2)}, u32[]{:S(2)}) collective-permute-start(bf16[1,64,1536]{2,1,0:T(8,128)(2,1)S(1)} %maximum_bitcast_fusion), channel_id=1, source_target_pairs={{384,0},{448,64},{0,128},{64,192},{128,256},{192,320},{256,384},{3... | collective-permute-start | bytes 589832 | tf_op jit(solution)/shard_map/ppermute | solution.py:207
  95.3 16.6 %collective-permute-start.2 = (bf16[1,64,1536]{2,1,0:T(8,128)(2,1)S(1)}, bf16[1,64,1536]{2,1,0:T(8,128)(2,1)S(1)}, u32[]{:S(2)}, u32[]{:S(2)}) collective-permute-start(bf16[1,64,1536]{2,1,0:T(8,128)(2,1)S(1)} %maximum_bitcast_fusion), channel_id=1, source_target_pairs={{128,0},{192,64},{256,128},{320,192},{384,256},{448,320},{0,384},{... | collective-permute-start | bytes 589832 | tf_op jit(solution)/shard_map/ppermute | solution.py:207
  99.5 17.8 %collective-permute-start.4 = (bf16[1,64,1536]{2,1,0:T(8,128)(2,1)S(1)}, bf16[1,64,1536]{2,1,0:T(8,128)(2,1)S(1)}, u32[]{:S(2)}, u32[]{:S(2)}) collective-permute-start(bf16[1,64,1536]{2,1,0:T(8,128)(2,1)S(1)} %maximum_bitcast_fusion), channel_id=1, source_target_pairs={{256,0},{320,64},{384,128},{448,192},{0,256},{64,320},{128,384},{1... | collective-permute-start | bytes 589832 | tf_op jit(solution)/shard_map/ppermute | solution.py:207
  112.0 12.1 %collective-permute-start.6 = (bf16[2,64,1536]{2,1,0:T(8,128)(2,1)S(1)}, bf16[2,64,1536]{2,1,0:T(8,128)(2,1)S(1)}, u32[]{:S(2)}, u32[]{:S(2)}) collective-permute-start(bf16[2,64,1536]{2,1,0:T(8,128)(2,1)S(1)} %get-tuple-element.11), channel_id=1, source_target_pairs={{64,0},{128,64},{192,128},{256,192},{320,256},{384,320},{448,384},... | collective-permute-start | bytes 1179656 | tf_op jit(solution)/shard_map/ppermute | solution.py:207
  113.9 13.7 %collective-permute-start.7 = (bf16[2,64,1536]{2,1,0:T(8,128)(2,1)S(1)}, bf16[2,64,1536]{2,1,0:T(8,128)(2,1)S(1)}, u32[]{:S(2)}, u32[]{:S(2)}) collective-permute-start(bf16[2,64,1536]{2,1,0:T(8,128)(2,1)S(1)} %get-tuple-element.10), channel_id=1, source_target_pairs={{448,0},{0,64},{64,128},{128,192},{192,256},{256,320},{320,384},{3... | collective-permute-start | bytes 1179656 | tf_op jit(solution)/shard_map/ppermute | solution.py:207
  117.4 14.0 %collective-permute-start.5 = (bf16[4,64,1536]{2,1,0:T(8,128)(2,1)S(1)}, bf16[4,64,1536]{2,1,0:T(8,128)(2,1)S(1)}, u32[]{:S(2)}, u32[]{:S(2)}) collective-permute-start(bf16[4,64,1536]{2,1,0:T(8,128)(2,1)S(1)} %pad_maximum_fusion.near), channel_id=1, source_target_pairs={{0,32},{32,0},{1,33},{33,1},{2,34},{34,2},{3,35},{35,3},{4,36},{36... | collective-permute-start | bytes 2359304 | tf_op jit(solution)/shard_map/ppermute | solution.py:211
  127.6 5.7 %collective-permute-start.8 = (bf16[4,64,1536]{2,1,0:T(8,128)(2,1)S(1)}, bf16[4,64,1536]{2,1,0:T(8,128)(2,1)S(1)}, u32[]{:S(2)}, u32[]{:S(2)}) collective-permute-start(bf16[4,64,1536]{2,1,0:T(8,128)(2,1)S(1)} %constant_dynamic-update-slice_fusion.odd), channel_id=1, source_target_pairs={{0,32},{32,0},{1,33},{33,1},{2,34},{34,2},{3,35},{35,3},{4,36},{36... | collective-permute-start | bytes 2359304 | tf_op jit(solution)/shard_map/ppermute | solution.py:211
  134.9 1.3 copy-start.1
  136.2 1.0 copy-start.2

commit v3 on v2

--- a/solution.py
+++ b/solution.py
@@ -221,9 +221,11 @@
     part = column_tiles(panel, col, rows, cols)
     factor = copies_for(inverse_factor.T, COL)
     factor = exchanged(factor, COL)
+    factor = factor.reshape(order, -1).T
+    packed = jnp.concatenate([factor, *part], axis=1)[None]
+
     copies = copies_for(panel, COL)
-    copies, factor = lax.optimization_barrier((copies, factor))
-    packed = jnp.concatenate([factor.reshape(order, -1).T, *part], axis=1)[None]
+    copies, packed = lax.optimization_barrier((copies, packed))
     full = exchanged(copies, COL)
     above = from_level(packed, 2)
     below = from_level(packed, 6)

time: 145 us -> 106 us (0.73)
  the two profiles are of different devices: /device:TPU:47 before, /device:TPU:1 now
where the time goes in v3:
time: 106 us; the launch traced here: 105 us
  starting transfers between devices  60.8 us (57%)
  waiting for transfers between devices  28.3 us (27%)
  Pallas kernels  9.07 us (9%)
  local copies, waits for them, and re-layouts  5.96 us (6%)
    all_to_all x2, starting transfers between devices, exchanged(): return lax.all_to_all(copies, axes, split_axis=0, concat_axis=0, tiled=True)  22.2 us
    ppermute x5, starting transfers between devices, from_level(): lax.ppermute(value, 'z', [((z + shift) % levels, z) for z in range(levels)])  22.1 us
    ppermute x5, waiting for transfers between devices, from_level(): lax.ppermute(value, 'z', [((z + shift) % levels, z) for z in range(levels)])  15.2 us
    all_to_all x2, waiting for transfers between devices, exchanged(): return lax.all_to_all(copies, axes, split_axis=0, concat_axis=0, tiled=True)  9.1 us
    pallas_call x1, Pallas kernels, solve_rows(): pl.pallas_call(row_kernel, out_shape=(jax.ShapeDtypeStruct((tiles, depth,...  7.47 us
    ppermute x2, starting transfers between devices, other_core(): return lax.ppermute(value, 'core', [(0, 1), (1, 0)])  7.43 us
    ppermute x1, starting transfers between devices, column_tiles(): moved = lax.ppermute(panel, ALL, moves)  5.73 us
    unnamed x14, local copies, waits for them, and re-layouts  3.43 us
  transfers between devices with their start and end apart: 11, of which 6 were waited for; matrix products, arithmetic and copies ran while one was open for 2% of the time, Pallas kernels for 2%

profile of v3, /device:TPU:1, one launch (start us, length us, event | category | flops | bytes accessed | tf_op | source)
XLA Modules:
  0.0 105.1 jit_solution(10549879226782817317)
XLA Ops:
  0.6 5.7 %collective-permute-start = (bf16[4,32,256]{2,1,0:T(8,128)(2,1)}, bf16[4,32,256]{2,1,0:T(8,128)(2,1)S(1)}, u32[]{:S(2)}, u32[]{:S(2)}) collective-permute-start(bf16[4,32,256]{2,1,0:T(8,128)(2,1)} %param.3), channel_id=1, source_target_pairs={{0,0},{1,1},{2,32},{3,33},{4,64},{5,65},{6,96},{7,97},{8,128},{9,1... | collective-permute-start | bytes 196616 | tf_op jit(solution)/shard_map/ppermute | solution.py:37
  6.4 2.1 %collective-permute-done = bf16[4,32,256]{2,1,0:T(8,128)(2,1)S(1)} collective-permute-done((bf16[4,32,256]{2,1,0:T(8,128)(2,1)}, bf16[4,32,256]{2,1,0:T(8,128)(2,1)S(1)}, u32[]{:S(2)}, u32[]{:S(2)}) %collective-permute-start) | collective-permute-done | bytes 65568 | tf_op jit(solution)/shard_map/ppermute | solution.py:37
  8.5 3.3 %collective-permute-start.1 = (bf16[2,32,256]{2,1,0:T(8,128)(2,1)S(1)}, bf16[2,32,256]{2,1,0:T(8,128)(2,1)S(1)}, u32[]{:S(2)}, u32[]{:S(2)}) collective-permute-start(bf16[2,32,256]{2,1,0:T(8,128)(2,1)S(1)} %constant_dynamic-slice_fusion), channel_id=1, source_target_pairs={{0,1},{1,0},{2,3},{3,2},{4,5},{5,4},{6,7},{7,6},{8,9},{9,8},{10,11... | collective-permute-start | bytes 98312 | tf_op jit(solution)/shard_map/ppermute | solution.py:40
  11.8 0.7 broadcast_in_dim.10
  12.6 0.8 reshape.8
  13.4 17.5 %all-to-all-start = ((bf16[32,2,1024]{2,1,0:T(2,128)(2,1)}), bf16[32,2,1024]{2,1,0:T(2,128)(2,1)S(1)}, u32[]{:S(2)}, u32[]{:S(2)}) async-start(bf16[32,2,1024]{2,1,0:T(2,128)(2,1)} %reshape.8), calls=%async_computation | async-start | bytes 262144 | tf_op jit(solution)/shard_map/all_to_all | solution.py:28
  30.9 0.0 collective-permute-done.1
  31.0 9.1 %all-to-all-done = bf16[32,2,1024]{2,1,0:T(2,128)(2,1)S(1)} async-done(((bf16[32,2,1024]{2,1,0:T(2,128)(2,1)}), bf16[32,2,1024]{2,1,0:T(2,128)(2,1)S(1)}, u32[]{:S(2)}, u32[]{:S(2)}) %all-to-all-start) | async-done | bytes 131104 | tf_op jit(solution)/shard_map/all_to_all | solution.py:28
  40.1 0.2 reshape.9
  40.3 0.1 copy.6
  40.5 1.6 %broadcast_in_dim.9 = bf16[32,4,32,256]{3,2,1,0:T(8,128)(2,1)} broadcast(bf16[4,32,256]{2,1,0:T(8,128)(2,1)S(1)} %copy-done.3), dimensions={1,2,3} | broadcast | bytes 2162688 | tf_op jit(solution)/shard_map/broadcast_in_dim | solution.py:24
  42.1 4.8 %all-to-all-start.1 = ((bf16[32,4,32,256]{3,2,1,0:T(8,128)(2,1)}), bf16[32,4,32,256]{3,2,1,0:T(8,128)(2,1)}, u32[]{:S(2)}, u32[]{:S(2)}) async-start(bf16[32,4,32,256]{3,2,1,0:T(8,128)(2,1)} %broadcast_in_dim.9), calls=%async_computation.1 | async-start | bytes 4194304 | tf_op jit(solution)/shard_map/all_to_all | solution.py:28
  46.8 8.2 %collective-permute-start.4 = (bf16[1,64,1536]{2,1,0:T(8,128)(2,1)S(1)}, bf16[1,64,1536]{2,1,0:T(8,128)(2,1)S(1)}, u32[]{:S(2)}, u32[]{:S(2)}) collective-permute-start(bf16[1,64,1536]{2,1,0:T(8,128)(2,1)S(1)} %maximum_bitcast_fusion), channel_id=1, source_target_pairs={{256,0},{320,64},{384,128},{448,192},{0,256},{64,320},{128,384},{1... | collective-permute-start | bytes 589832 | tf_op jit(solution)/shard_map/ppermute | solution.py:207
  55.1 4.8 %collective-permute-start.3 = (bf16[1,64,1536]{2,1,0:T(8,128)(2,1)S(1)}, bf16[1,64,1536]{2,1,0:T(8,128)(2,1)S(1)}, u32[]{:S(2)}, u32[]{:S(2)}) collective-permute-start(bf16[1,64,1536]{2,1,0:T(8,128)(2,1)S(1)} %maximum_bitcast_fusion), channel_id=1, source_target_pairs={{384,0},{448,64},{0,128},{64,192},{128,256},{192,320},{256,384},{3... | collective-permute-start | bytes 589832 | tf_op jit(solution)/shard_map/ppermute | solution.py:207
  59.9 2.6 %collective-permute-start.2 = (bf16[1,64,1536]{2,1,0:T(8,128)(2,1)S(1)}, bf16[1,64,1536]{2,1,0:T(8,128)(2,1)S(1)}, u32[]{:S(2)}, u32[]{:S(2)}) collective-permute-start(bf16[1,64,1536]{2,1,0:T(8,128)(2,1)S(1)} %maximum_bitcast_fusion), channel_id=1, source_target_pairs={{128,0},{192,64},{256,128},{320,192},{384,256},{448,320},{0,384},{... | collective-permute-start | bytes 589832 | tf_op jit(solution)/shard_map/ppermute | solution.py:207
  62.5 0.0 copy-start
  62.5 4.9 %collective-permute-done.3 = bf16[1,64,1536]{2,1,0:T(8,128)(2,1)S(1)} collective-permute-done((bf16[1,64,1536]{2,1,0:T(8,128)(2,1)S(1)}, bf16[1,64,1536]{2,1,0:T(8,128)(2,1)S(1)}, u32[]{:S(2)}, u32[]{:S(2)}) %collective-permute-start.3) | collective-permute-done | bytes 196640 | tf_op jit(solution)/shard_map/ppermute | solution.py:207
  67.4 6.6 %collective-permute-done.2 = bf16[1,64,1536]{2,1,0:T(8,128)(2,1)S(1)} collective-permute-done((bf16[1,64,1536]{2,1,0:T(8,128)(2,1)S(1)}, bf16[1,64,1536]{2,1,0:T(8,128)(2,1)S(1)}, u32[]{:S(2)}, u32[]{:S(2)}) %collective-permute-start.2) | collective-permute-done | bytes 196640 | tf_op jit(solution)/shard_map/ppermute | solution.py:207
  74.0 0.1 pad_maximum_fusion
  74.1 2.3 %collective-permute-start.7 = (bf16[2,64,1536]{2,1,0:T(8,128)(2,1)S(1)}, bf16[2,64,1536]{2,1,0:T(8,128)(2,1)S(1)}, u32[]{:S(2)}, u32[]{:S(2)}) collective-permute-start(bf16[2,64,1536]{2,1,0:T(8,128)(2,1)S(1)} %get-tuple-element.10), channel_id=1, source_target_pairs={{448,0},{0,64},{64,128},{128,192},{192,256},{256,320},{320,384},{3... | collective-permute-start | bytes 1179656 | tf_op jit(solution)/shard_map/ppermute | solution.py:207
  76.4 4.2 %collective-permute-start.6 = (bf16[2,64,1536]{2,1,0:T(8,128)(2,1)S(1)}, bf16[2,64,1536]{2,1,0:T(8,128)(2,1)S(1)}, u32[]{:S(2)}, u32[]{:S(2)}) collective-permute-start(bf16[2,64,1536]{2,1,0:T(8,128)(2,1)S(1)} %get-tuple-element.11), channel_id=1, source_target_pairs={{64,0},{128,64},{192,128},{256,192},{320,256},{384,320},{448,384},... | collective-permute-start | bytes 1179656 | tf_op jit(solution)/shard_map/ppermute | solution.py:207
  80.6 0.0 collective-permute-done.4
  80.6 3.8 %collective-permute-start.5 = (bf16[4,64,1536]{2,1,0:T(8,128)(2,1)S(1)}, bf16[4,64,1536]{2,1,0:T(8,128)(2,1)S(1)}, u32[]{:S(2)}, u32[]{:S(2)}) collective-permute-start(bf16[4,64,1536]{2,1,0:T(8,128)(2,1)S(1)} %constant_dynamic-update-slice_fusion.near), channel_id=1, source_target_pairs={{0,32},{32,0},{1,33},{33,1},{2,34},{34,2},{3,35},{35,3},{4,36},{36... | collective-permute-start | bytes 2359304 | tf_op jit(solution)/shard_map/ppermute | solution.py:211
  84.4 3.7 %collective-permute-done.6 = bf16[2,64,1536]{2,1,0:T(8,128)(2,1)S(1)} collective-permute-done((bf16[2,64,1536]{2,1,0:T(8,128)(2,1)S(1)}, bf16[2,64,1536]{2,1,0:T(8,128)(2,1)S(1)}, u32[]{:S(2)}, u32[]{:S(2)}) %collective-permute-start.6) | collective-permute-done | bytes 393248 | tf_op jit(solution)/shard_map/ppermute | solution.py:207
  88.2 0.0 collective-permute-done.7
  88.2 3.7 %collective-permute-start.8 = (bf16[4,64,1536]{2,1,0:T(8,128)(2,1)S(1)}, bf16[4,64,1536]{2,1,0:T(8,128)(2,1)S(1)}, u32[]{:S(2)}, u32[]{:S(2)}) collective-permute-start(bf16[4,64,1536]{2,1,0:T(8,128)(2,1)S(1)} %constant_dynamic-update-slice_fusion.4.odd), channel_id=1, source_target_pairs={{0,32},{32,0},{1,33},{33,1},{2,34},{34,2},{3,35},{35,3},{4,36},{36... | collective-permute-start | bytes 2359304 | tf_op jit(solution)/shard_map/ppermute | solution.py:211
  91.9 1.9 %collective-permute-done.8.odd_core = bf16[4,64,1536]{2,1,0:T(8,128)(2,1)S(1)} collective-permute-done((bf16[4,64,1536]{2,1,0:T(8,128)(2,1)S(1)}, bf16[4,64,1536]{2,1,0:T(8,128)(2,1)S(1)}, u32[]{:S(2)}, u32[]{:S(2)}) %collective-permute-start.8) | collective-permute-done | bytes 786464 | tf_op jit(solution)/shard_map/ppermute | solution.py:211
  93.8 1.6 %shard_map.50 = (bf16[1024,1024]{1,0:T(8,128)(2,1)S(1)}, bf16[1024,512]{1,0:T(8,128)(2,1)S(1)}) custom-call(s32[64]{0:T(128)S(1)} %copy-done, bf16[4,64,1536]{2,1,0:T(8,128)(2,1)S(1)} %constant_dynamic-update-slice_fusion.near, bf16[4,64,1536]{2,1,0:T(8,128)(2,1)S(1)} %collective-permute-done.5.near_core, ...), custom_call_target="tpu_custom_call" | custom-call | flops 1073741824 | bytes 6291456 | tf_op jit(solution)/shard_map/pallas_call | solution.py:101
  95.4 1.3 %copy-done.1 = bf16[1024,1024]{1,0:T(8,128)(2,1)} copy-done((bf16[1024,1024]{1,0:T(8,128)(2,1)}, bf16[1024,1024]{1,0:T(8,128)(2,1)S(1)}, u32[]{:S(2)}) %copy-start.1) | copy-done | bytes 2097176
  96.7 1.0 copy-done.2
  97.6 0.0 all-to-all-done.1.full
  97.7 7.5 %shard_map.51 = (bf16[4,32,256]{2,1,0:T(8,128)(2,1)}, bf16[4,2,256,256]{3,2,1,0:T(8,128)(2,1)}) custom-call(s32[64]{0:T(128)} %ranks.3, bf16[1024,1024]{1,0:T(8,128)(2,1)} %copy-done.1, bf16[1024,512]{1,0:T(8,128)(2,1)} %copy-done.2, bf16[32,4,32,256]{3,2,1,0:T(8,128)(2,1)} %all-to-all-done.1.full), custom_call_target="tpu_custom_call" | custom-call | flops 3221225472 | bytes 6291456 | tf_op jit(solution)/shard_map/pallas_call | solution.py:182
  (16 shorter events, 0.2 us)
Async XLA Ops:
  0.6 39.8 %copy-start.3 = (bf16[4,32,256]{2,1,0:T(8,128)(2,1)S(1)}, bf16[4,32,256]{2,1,0:T(8,128)(2,1)}, u32[]{:S(2)}) copy-start(bf16[4,32,256]{2,1,0:T(8,128)(2,1)} %param.3) | copy-start | bytes 196612
  0.6 7.9 %collective-permute-start = (bf16[4,32,256]{2,1,0:T(8,128)(2,1)}, bf16[4,32,256]{2,1,0:T(8,128)(2,1)S(1)}, u32[]{:S(2)}, u32[]{:S(2)}) collective-permute-start(bf16[4,32,256]{2,1,0:T(8,128)(2,1)} %param.3), channel_id=1, source_target_pairs={{0,0},{1,1},{2,32},{3,33},{4,64},{5,65},{6,96},{7,97},{8,128},{9,1... | collective-permute-start | bytes 196616 | tf_op jit(solution)/shard_map/ppermute | solution.py:37
  8.5 22.4 %collective-permute-start.1 = (bf16[2,32,256]{2,1,0:T(8,128)(2,1)S(1)}, bf16[2,32,256]{2,1,0:T(8,128)(2,1)S(1)}, u32[]{:S(2)}, u32[]{:S(2)}) collective-permute-start(bf16[2,32,256]{2,1,0:T(8,128)(2,1)S(1)} %constant_dynamic-slice_fusion), channel_id=1, source_target_pairs={{0,1},{1,0},{2,3},{3,2},{4,5},{5,4},{6,7},{7,6},{8,9},{9,8},{10,11... | collective-permute-start | bytes 98312 | tf_op jit(solution)/shard_map/ppermute | solution.py:40
  13.4 26.6 %all-to-all-start = ((bf16[32,2,1024]{2,1,0:T(2,128)(2,1)}), bf16[32,2,1024]{2,1,0:T(2,128)(2,1)S(1)}, u32[]{:S(2)}, u32[]{:S(2)}) async-start(bf16[32,2,1024]{2,1,0:T(2,128)(2,1)} %reshape.8), calls=%async_computation | async-start | bytes 262144 | tf_op jit(solution)/shard_map/all_to_all | solution.py:28
  42.1 55.6 %all-to-all-start.1 = ((bf16[32,4,32,256]{3,2,1,0:T(8,128)(2,1)}), bf16[32,4,32,256]{3,2,1,0:T(8,128)(2,1)}, u32[]{:S(2)}, u32[]{:S(2)}) async-start(bf16[32,4,32,256]{3,2,1,0:T(8,128)(2,1)} %broadcast_in_dim.9), calls=%async_computation.1 | async-start | bytes 4194304 | tf_op jit(solution)/shard_map/all_to_all | solution.py:28
  46.8 33.8 %collective-permute-start.4 = (bf16[1,64,1536]{2,1,0:T(8,128)(2,1)S(1)}, bf16[1,64,1536]{2,1,0:T(8,128)(2,1)S(1)}, u32[]{:S(2)}, u32[]{:S(2)}) collective-permute-start(bf16[1,64,1536]{2,1,0:T(8,128)(2,1)S(1)} %maximum_bitcast_fusion), channel_id=1, source_target_pairs={{256,0},{320,64},{384,128},{448,192},{0,256},{64,320},{128,384},{1... | collective-permute-start | bytes 589832 | tf_op jit(solution)/shard_map/ppermute | solution.py:207
  55.1 12.4 %collective-permute-start.3 = (bf16[1,64,1536]{2,1,0:T(8,128)(2,1)S(1)}, bf16[1,64,1536]{2,1,0:T(8,128)(2,1)S(1)}, u32[]{:S(2)}, u32[]{:S(2)}) collective-permute-start(bf16[1,64,1536]{2,1,0:T(8,128)(2,1)S(1)} %maximum_bitcast_fusion), channel_id=1, source_target_pairs={{384,0},{448,64},{0,128},{64,192},{128,256},{192,320},{256,384},{3... | collective-permute-start | bytes 589832 | tf_op jit(solution)/shard_map/ppermute | solution.py:207
  59.9 14.1 %collective-permute-start.2 = (bf16[1,64,1536]{2,1,0:T(8,128)(2,1)S(1)}, bf16[1,64,1536]{2,1,0:T(8,128)(2,1)S(1)}, u32[]{:S(2)}, u32[]{:S(2)}) collective-permute-start(bf16[1,64,1536]{2,1,0:T(8,128)(2,1)S(1)} %maximum_bitcast_fusion), channel_id=1, source_target_pairs={{128,0},{192,64},{256,128},{320,192},{384,256},{448,320},{0,384},{... | collective-permute-start | bytes 589832 | tf_op jit(solution)/shard_map/ppermute | solution.py:207
  62.5 31.3 %copy-start = (s32[64]{0:T(128)S(1)}, s32[64]{0:T(128)}, u32[]{:S(2)}) copy-start(s32[64]{0:T(128)} %ranks.3) | copy-start | bytes 772
  74.1 14.1 %collective-permute-start.7 = (bf16[2,64,1536]{2,1,0:T(8,128)(2,1)S(1)}, bf16[2,64,1536]{2,1,0:T(8,128)(2,1)S(1)}, u32[]{:S(2)}, u32[]{:S(2)}) collective-permute-start(bf16[2,64,1536]{2,1,0:T(8,128)(2,1)S(1)} %get-tuple-element.10), channel_id=1, source_target_pairs={{448,0},{0,64},{64,128},{128,192},{192,256},{256,320},{320,384},{3... | collective-permute-start | bytes 1179656 | tf_op jit(solution)/shard_map/ppermute | solution.py:207
  76.4 11.8 %collective-permute-start.6 = (bf16[2,64,1536]{2,1,0:T(8,128)(2,1)S(1)}, bf16[2,64,1536]{2,1,0:T(8,128)(2,1)S(1)}, u32[]{:S(2)}, u32[]{:S(2)}) collective-permute-start(bf16[2,64,1536]{2,1,0:T(8,128)(2,1)S(1)} %get-tuple-element.11), channel_id=1, source_target_pairs={{64,0},{128,64},{192,128},{256,192},{320,256},{384,320},{448,384},... | collective-permute-start | bytes 1179656 | tf_op jit(solution)/shard_map/ppermute | solution.py:207
  80.6 11.2 %collective-permute-start.5 = (bf16[4,64,1536]{2,1,0:T(8,128)(2,1)S(1)}, bf16[4,64,1536]{2,1,0:T(8,128)(2,1)S(1)}, u32[]{:S(2)}, u32[]{:S(2)}) collective-permute-start(bf16[4,64,1536]{2,1,0:T(8,128)(2,1)S(1)} %constant_dynamic-update-slice_fusion.near), channel_id=1, source_target_pairs={{0,32},{32,0},{1,33},{33,1},{2,34},{34,2},{3,35},{35,3},{4,36},{36... | collective-permute-start | bytes 2359304 | tf_op jit(solution)/shard_map/ppermute | solution.py:211
  88.2 5.6 %collective-permute-start.8 = (bf16[4,64,1536]{2,1,0:T(8,128)(2,1)S(1)}, bf16[4,64,1536]{2,1,0:T(8,128)(2,1)S(1)}, u32[]{:S(2)}, u32[]{:S(2)}) collective-permute-start(bf16[4,64,1536]{2,1,0:T(8,128)(2,1)S(1)} %constant_dynamic-update-slice_fusion.4.odd), channel_id=1, source_target_pairs={{0,32},{32,0},{1,33},{33,1},{2,34},{34,2},{3,35},{35,3},{4,36},{36... | collective-permute-start | bytes 2359304 | tf_op jit(solution)/shard_map/ppermute | solution.py:211
  95.4 1.3 %copy-start.1 = (bf16[1024,1024]{1,0:T(8,128)(2,1)}, bf16[1024,1024]{1,0:T(8,128)(2,1)S(1)}, u32[]{:S(2)}) copy-start(bf16[1024,1024]{1,0:T(8,128)(2,1)S(1)} %get-tuple-element.7.factor_in) | copy-start | bytes 6291460
  96.7 1.0 copy-start.2
